TPU v7x, 256 devices: a whole 4x4x8 slice. The times are simulated.
256 devices in a mesh: row: 16 (over z, x_lo), col: 16 (over y, x_hi, core).
Axes of the slice: x: 4 (x_hi: 2, x_lo: 2; x = x_hi * 2 + x_lo), y: 4, z: 8, core: 2. Of those that a mesh axis runs over, the one named last changes fastest.
Arguments:
- pair: bfloat16 [512, 512, 128], P('row', 'col'), may hold values from -6 to 6
- pair_mask: int32 [512, 512], P('row', 'col'), may hold values from 0 to 1, as said below
- proj_weight: bfloat16 [128, 640], replicated, may hold values from -0.5 to 0.5
- out_weight: bfloat16 [128, 128], replicated, may hold values from -0.5 to 0.5
- in_gain: float32 [128], replicated, may hold values from 0.5 to 1.5
- out_gain: float32 [128], replicated, may hold values from 0.5 to 1.5
- cotangent: bfloat16 [512, 512, 128], P('row', 'col'), may hold values from -6 to 6
Outputs:
- d_pair: float32 [512, 512, 128], P('row', 'col')
- d_proj_weight: float32 [128, 640], replicated
- d_out_weight: float32 [128, 128], replicated
- d_in_gain: float32 [128], replicated
- d_out_gain: float32 [128], replicated
Inputs may be any that keep to these rules, and one draw needn't show every extreme that they name: pair_mask[i, j] is the product of a 0/1 flag of token i and the same flag of token j.
All inputs are finite; a program needn't handle non-finite values.
Results may differ from a plain program's by a relative error of at most 0.019.
Values may be sent and summed in bfloat16 or wider, within the bound.
A program may use at most 128 MiB of HBM per device.

v0:
```python
import jax
import jax.numpy as jnp
from jax import lax
from jax.sharding import PartitionSpec as P


def normalize(values):
    average = jnp.mean(values, axis=-1, keepdims=True)
    centred = values - average
    spread = jnp.mean(centred * centred, axis=-1, keepdims=True)
    inverse = lax.rsqrt(spread + 1e-05)
    return (centred * inverse, inverse)


def layer_back(grad_hat, normed, inverse):
    first_mean = jnp.mean(grad_hat, axis=-1, keepdims=True)
    second_mean = jnp.mean(grad_hat * normed, axis=-1, keepdims=True)
    return (grad_hat - first_mean - normed * second_mean) * inverse


def body(pair, pair_mask, proj_weight, out_weight, in_gain, out_gain, cotangent):
    tile_rows = pair.shape[0]
    channels = pair.shape[2]
    row_count = lax.axis_size("row")
    total = tile_rows * row_count
    normed, inverse = normalize(pair.astype(jnp.float32))
    zn = (normed * in_gain).astype(jnp.bfloat16)
    linear = jnp.einsum("ijc,ce->ije", zn, proj_weight, preferred_element_type=jnp.float32)
    proj_left = linear[..., 0:channels]
    gate_left = linear[..., channels : 2 * channels]
    proj_right = linear[..., 2 * channels : 3 * channels]
    gate_right = linear[..., 3 * channels : 4 * channels]
    gate_out = linear[..., 4 * channels :]
    mask_f = pair_mask.astype(jnp.float32)[..., None]
    sig_left = jax.nn.sigmoid(gate_left)
    sig_right = jax.nn.sigmoid(gate_right)
    left = (mask_f * sig_left * proj_left).astype(jnp.bfloat16)
    right = (mask_f * sig_right * proj_right).astype(jnp.bfloat16)
    panels = lax.all_gather(left, "col", axis=1, tiled=True)
    piece = panels
    triangle = lax.psum_scatter(
        jnp.einsum("kic,kjc->ijc", piece, right, preferred_element_type=jnp.float32).astype(
            jnp.bfloat16
        ),
        "row",
        scatter_dimension=0,
        tiled=True,
    ).astype(jnp.float32)
    tri_hat, tri_inv = normalize(triangle)
    onorm = (tri_hat * out_gain).astype(jnp.bfloat16)
    projected = jnp.einsum("ijc,cd->ijd", onorm, out_weight, preferred_element_type=jnp.float32)
    sig_gate = jax.nn.sigmoid(gate_out)
    cot_f = cotangent.astype(jnp.float32)
    dproj = (cot_f * sig_gate).astype(jnp.bfloat16)
    dgate = cot_f * projected * sig_gate * (1.0 - sig_gate)
    out_weight_local = jnp.einsum("ijc,ijd->cd", onorm, dproj, preferred_element_type=jnp.float32)
    donorm = jnp.einsum("ijd,cd->ijc", dproj, out_weight, preferred_element_type=jnp.float32)
    out_gain_local = jnp.sum(donorm * tri_hat, axis=(0, 1))
    dtri = layer_back(donorm * out_gain, tri_hat, tri_inv).astype(jnp.bfloat16)
    do_panels = lax.all_gather(dtri, "row", axis=0, tiled=True)
    piece = do_panels
    dleft = jnp.transpose(
        lax.psum_scatter(
            jnp.einsum("ijc,kjc->ikc", piece, right, preferred_element_type=jnp.float32).astype(
                jnp.bfloat16
            ),
            "col",
            scatter_dimension=0,
            tiled=True,
        ).astype(jnp.float32),
        (1, 0, 2),
    )
    dright = jnp.einsum("kic,ijc->kjc", panels, do_panels, preferred_element_type=jnp.float32)
    dlin = jnp.concatenate(
        [
            dleft * mask_f * sig_left,
            dleft * mask_f * proj_left * sig_left * (1.0 - sig_left),
            dright * mask_f * sig_right,
            dright * mask_f * proj_right * sig_right * (1.0 - sig_right),
            dgate,
        ],
        axis=-1,
    ).astype(jnp.bfloat16)
    proj_local = jnp.einsum("ijc,ije->ce", zn, dlin, preferred_element_type=jnp.float32)
    dzn = jnp.einsum("ije,ce->ijc", dlin, proj_weight, preferred_element_type=jnp.float32)
    in_gain_local = jnp.sum(dzn * normed, axis=(0, 1))
    d_pair = layer_back(dzn * in_gain, normed, inverse)
    proj_sum, out_weight_sum, in_gain_sum, out_gain_sum = lax.psum(
        (proj_local, out_weight_local, in_gain_local, out_gain_local), ("row", "col")
    )
    return (
        d_pair,
        proj_sum / total,
        out_weight_sum / total,
        in_gain_sum / total,
        out_gain_sum / total,
    )


def solution(mesh):
    in_specs = (P("row", "col", None), P("row", "col"), P(), P(), P(), P(), P("row", "col", None))
    out_specs = (P("row", "col", None), P(), P(), P(), P())
    return jax.shard_map(body, mesh=mesh, in_specs=in_specs, out_specs=out_specs, check_vma=False)
```

profile of v0, /device:TPU:1, one launch (start us, length us, event | category | flops | bytes accessed | tf_op | source)
XLA Modules:
  0.0 758.8 jit_solution(18180384380420288592)
XLA Ops:
  7.2 0.0 copy-start
  7.2 0.0 copy-start.6
  7.2 0.0 all-gather.3.cloned.1.call-start
  7.2 0.8 convert_element_type.44
  8.0 1.2 convert_reduce_fusion.1
  9.2 1.3 fusion.28
  10.5 0.0 copy-done
  10.6 1.6 fusion.51
  12.1 0.0 copy-done.6
  12.1 1.2 multiply_convert_fusion.2
  13.3 0.0 all-gather.3.cloned.1.call-update
  13.3 0.0 reduce-scatter.3.cloned.1.call-start
  13.4 2.3 copy.24
  15.7 63.4 %all-gather.3.cloned.1.call-done = bf16[32,512,128]{2,1,0:T(8,128)(2,1)} async-done(((bf16[32,32,128]{2,1,0:T(8,128)(2,1)}), bf16[32,512,128]{2,1,0:T(8,128)(2,1)}) %all-gather.3.cloned.1.call-update) | async-done | bytes 4194320 | tf_op jit(solution)/shard_map/all_gather | solution.py:39
  79.1 8.0 %copy.22 = bf16[32,512,128]{1,0,2:T(8,128)(2,1)} copy(bf16[32,512,128]{2,1,0:T(8,128)(2,1)} %all-gather.3.cloned.1.call-done) | data formatting | bytes 8388608 | tf_op jit(solution)/shard_map/all_gather | solution.py:39
  87.1 5.8 fusion.60
  92.9 9.2 %copy.23 = bf16[128,32,512]{0,1,2:T(8,128)(2,1)} copy(bf16[128,32,512]{2,1,0:T(8,128)(2,1)} %fusion.60) | data formatting | bytes 8388608 | tf_op jit(solution)/shard_map/kic,kjc->ijc/dot_general | solution.py:42
  102.0 0.0 reduce-scatter.3.cloned.1.call-update
  102.1 0.0 all-gather.5.cloned.1.call-start
  102.1 95.7 %reduce-scatter.3.cloned.1.call-done = bf16[32,32,128]{2,1,0:T(8,128)(2,1)} async-done(((bf16[512,32,128]{2,1,0:T(8,128)(2,1)}), bf16[32,32,128]{2,1,0:T(8,128)(2,1)}) %reduce-scatter.3.cloned.1.call-update) | async-done | bytes 262160 | tf_op jit(solution)/shard_map/reduce_scatter | solution.py:41
  197.8 1.2 convert_reduce_fusion
  199.0 1.3 fusion.22
  200.3 0.0 copy-done.8
  200.3 0.0 copy-done.10
  200.4 0.0 copy-done.11
  200.4 1.6 fusion.21
  202.0 2.3 fusion.19
  204.3 0.0 all-gather.5.cloned.1.call-update
  204.3 0.0 reduce-scatter.5.cloned.1.call-start
  204.3 98.2 %all-gather.5.cloned.1.call-done = bf16[512,32,128]{2,1,0:T(8,128)(2,1)} async-done(((bf16[32,32,128]{2,1,0:T(8,128)(2,1)}), bf16[512,32,128]{2,1,0:T(8,128)(2,1)}) %all-gather.5.cloned.1.call-update) | async-done | bytes 4194320 | tf_op jit(solution)/shard_map/all_gather | solution.py:60
  302.6 8.6 %copy.27 = bf16[512,32,128]{0,1,2:T(8,128)(2,1)} copy(bf16[512,32,128]{2,1,0:T(8,128)(2,1)} %all-gather.5.cloned.1.call-done) | data formatting | bytes 8388608 | tf_op jit(solution)/shard_map/all_gather | solution.py:60
  311.2 5.7 fusion.61
  316.9 7.9 %copy.26 = bf16[128,32,512]{0,2,1:T(8,128)(2,1)} copy(bf16[128,32,512]{2,1,0:T(8,128)(2,1)} %fusion.61) | data formatting | bytes 8388608 | tf_op jit(solution)/shard_map/ijc,kjc->ikc/dot_general | solution.py:64
  324.8 0.0 reduce-scatter.5.cloned.1.call-update
  324.8 0.2 all-reduce.4.cloned.1.call-start
  325.0 0.7 copy-done.3
  325.7 1.2 convolution_bitcast_fusion.1
  326.9 6.1 fusion.62
  333.0 2.8 copy.29
  335.8 0.0 copy-start.2
  335.8 78.5 %reduce-scatter.5.cloned.1.call-done = bf16[32,32,128]{2,0,1:T(8,128)(2,1)} async-done(((bf16[512,32,128]{2,0,1:T(8,128)(2,1)}), bf16[32,32,128]{2,0,1:T(8,128)(2,1)}) %reduce-scatter.5.cloned.1.call-update) | async-done | bytes 262160 | tf_op jit(solution)/shard_map/reduce_scatter | solution.py:63
  414.3 1.1 fusion.48
  415.5 0.0 copy-start.4
  415.5 0.0 copy-start.7
  415.5 1.3 fusion.47
  416.8 0.0 copy-done.2
  416.8 0.3 fusion.45
  417.1 0.0 copy-start.1
  417.1 0.0 copy-start.9
  417.1 1.4 fusion.46
  418.5 0.0 copy-done.4
  418.5 0.5 fusion.3
  419.0 1.1 copy-done.5
  420.1 0.0 copy-done.1
  420.1 1.5 convolution_bitcast_fusion
  421.6 2.1 fusion.27
  423.6 77.0 %all-reduce = (f32[128]{0:T(128)S(1)}, f32[128]{0:T(128)S(1)}) all-reduce(f32[128]{0:T(128)S(1)} %get-tuple-element.7, f32[128]{0:T(128)S(1)} %get-tuple-element.5), channel_id=1, replica_groups=mesh['row'=16,'col'=16] {'row','col'}, use_global_device_ids=true, to_apply=%region_13.0 | all-reduce | flops 256 | bytes 2048 | tf_op jit(solution)/shard_map/psum | solution.py:88
  500.6 0.5 broadcast_multiply_fusion.9
  501.1 0.0 all-reduce.4.cloned.1.call-update
  501.2 1.4 fusion.26
  502.6 0.5 broadcast_multiply_fusion.8
  503.1 246.0 %all-reduce.4.cloned.1.call-done = (f32[128,640]{1,0:T(8,128)}, f32[128,128]{1,0:T(8,128)}) async-done(((f32[128,640]{1,0:T(8,128)}, f32[128,128]{1,0:T(8,128)}), (f32[128,640]{1,0:T(8,128)}, f32[128,128]{1,0:T(8,128)})) %all-reduce.4.cloned.1.call-update) | async-done | bytes 393232 | tf_op jit(solution)/shard_map/psum | solution.py:88
  749.1 1.7 broadcast_multiply_fusion
  750.8 1.5 broadcast_multiply_fusion.1
  (14 shorter events, 0.1 us)
Async XLA Ops:
  7.2 3.4 copy-start
  7.2 4.9 copy-start.6
  7.2 71.9 %all-gather.3.cloned.1.call-start = ((), (), s32[]{:S(2)}) async-start(), calls=%async_computation.2 | async-start | bytes 4456448 | tf_op jit(solution)/shard_map/all_gather | solution.py:39
  13.3 184.5 %reduce-scatter.3.cloned.1.call-start = ((), (), s32[]{:S(2)}) async-start(), calls=%async_computation.3 | async-start | bytes 4456448 | tf_op jit(solution)/shard_map/reduce_scatter | solution.py:41
  102.0 98.3 %copy-start.8 = (bf16[32,32,128]{2,1,0:T(8,128)(2,1)S(1)}, bf16[32,32,128]{2,1,0:T(8,128)(2,1)}, u32[]{:S(2)}) copy-start(bf16[32,32,128]{2,1,0:T(8,128)(2,1)} %get-tuple-element.17) | copy-start | bytes 786436
  102.0 98.3 %copy-start.10 = (f32[128]{0:T(128)S(1)}, f32[128]{0:T(128)}, u32[]{:S(2)}) copy-start(f32[128]{0:T(128)} %param.12) | copy-start | bytes 1540
  102.0 98.3 %copy-start.11 = (bf16[128,128]{1,0:T(8,128)(2,1)S(1)}, bf16[128,128]{1,0:T(8,128)(2,1)}, u32[]{:S(2)}) copy-start(bf16[128,128]{1,0:T(8,128)(2,1)} %param.10) | copy-start | bytes 98308
  102.1 200.5 %all-gather.5.cloned.1.call-start = ((), (), s32[]{:S(2)}) async-start(), calls=%async_computation.4 | async-start | bytes 4456448 | tf_op jit(solution)/shard_map/all_gather | solution.py:60
  204.3 210.0 %reduce-scatter.5.cloned.1.call-start = ((), (), s32[]{:S(2)}) async-start(), calls=%async_computation.5 | async-start | bytes 4456448 | tf_op jit(solution)/shard_map/reduce_scatter | solution.py:63
  324.8 0.9 copy-start.3
  324.8 424.3 %all-reduce.4.cloned.1.call-start = ((), (), s32[]{:S(2)}) async-start(), calls=%async_computation.6 | async-start | bytes 786432 | tf_op jit(solution)/shard_map/psum | solution.py:88
  335.8 81.0 %copy-start.2 = (f32[128,32,32]{0,1,2:T(8,128)}, f32[128,32,32]{0,1,2:T(8,128)S(1)}, u32[]{:S(2)}) copy-start(f32[128,32,32]{0,1,2:T(8,128)S(1)} %copy.29) | copy-start | bytes 1572868
  415.5 3.0 copy-start.4
  415.5 3.0 copy-start.7
  417.1 3.0 copy-start.1
  417.1 3.0 copy-start.9
  419.0 1.1 copy-start.5
Sparse Core Ops, SparseCore 0:
  13.4 65.6 all-gather.2
  102.2 95.5 reduce-scatter.2
  204.4 98.1 all-gather.4
  324.9 89.3 reduce-scatter.4
  501.3 247.7 all-reduce.3
where the time goes:
time: 760 us; the launch traced here: 759 us
  waiting for transfers between devices  582 us (77%)
  blocking collectives  77 us (10%)
  local copies, waits for them, and re-layouts  40.6 us (5%)
  matrix products  26 us (3%)
  other arithmetic  18.9 us (2%)
  between operations  14 us (2%)
    psum x1, waiting for transfers between devices, body(): lax.psum((proj_local, out_weight_local, in_gain_local, out_gain_local), (...  246 us
    all_gather x1, waiting for transfers between devices, body(): do_panels = lax.all_gather(dtri, 'row', axis=0, tiled=True)  98.2 us
    reduce_scatter x1, waiting for transfers between devices, body(): lax.psum_scatter(jnp.einsum('kic,kjc->ijc', piece, right, preferred_eleme...  95.7 us
    reduce_scatter x1, waiting for transfers between devices, body(): lax.psum_scatter(jnp.einsum('ijc,kjc->ikc', piece, right, preferred_eleme...  78.5 us
    psum x1, blocking collectives, body(): lax.psum((proj_local, out_weight_local, in_gain_local, out_gain_local), (...  77 us
    all_gather x1, waiting for transfers between devices, body(): panels = lax.all_gather(left, 'col', axis=1, tiled=True)  63.4 us
  transfers between devices with their start and end apart: 5, of which 5 were waited for; matrix products, arithmetic and copies ran while one was open for 2% of the time, Pallas kernels for 0%

commit v1 on v0

--- a/solution.py
+++ b/solution.py
@@ -18,11 +18,21 @@
     return (grad_hat - first_mean - normed * second_mean) * inverse
 
 
+AXES = ("row", "col")
+
+
+def exchange(x):
+    return lax.all_to_all(x, AXES, split_axis=0, concat_axis=0, tiled=True)
+
+
 def body(pair, pair_mask, proj_weight, out_weight, in_gain, out_gain, cotangent):
-    tile_rows = pair.shape[0]
+    t = pair.shape[0]
+    half_t = t // 2
     channels = pair.shape[2]
-    row_count = lax.axis_size("row")
-    total = tile_rows * row_count
+    rows = lax.axis_size("row")
+    cols = lax.axis_size("col")
+    total = t * rows
+    half = lax.rem(lax.axis_index("col"), 2)
     normed, inverse = normalize(pair.astype(jnp.float32))
     zn = (normed * in_gain).astype(jnp.bfloat16)
     linear = jnp.einsum("ijc,ce->ije", zn, proj_weight, preferred_element_type=jnp.float32)
@@ -36,16 +46,29 @@
     sig_right = jax.nn.sigmoid(gate_right)
     left = (mask_f * sig_left * proj_left).astype(jnp.bfloat16)
     right = (mask_f * sig_right * proj_right).astype(jnp.bfloat16)
-    panels = lax.all_gather(left, "col", axis=1, tiled=True)
-    piece = panels
-    triangle = lax.psum_scatter(
-        jnp.einsum("kic,kjc->ijc", piece, right, preferred_element_type=jnp.float32).astype(
-            jnp.bfloat16
-        ),
-        "row",
-        scatter_dimension=0,
-        tiled=True,
-    ).astype(jnp.float32)
+
+    def out_full(x):
+        x = jnp.transpose(x, (2, 0, 1)).reshape(channels, 1, t * t)
+        return jnp.broadcast_to(x, (channels, 2, t * t)).reshape(2 * channels, t * t)
+
+    def matrix(x):
+        return (
+            x.reshape(rows, cols, t, t).transpose(0, 2, 1, 3).reshape(rows * t, cols * t)
+        )
+
+    def pick(x):
+        x = x.reshape(x.shape[0], -1, 2, half_t)
+        return lax.dynamic_index_in_dim(x, half, 2, keepdims=False).reshape(x.shape[0], -1)
+
+    sent = exchange(jnp.concatenate([out_full(left), out_full(right)], axis=1))
+    left_c = matrix(sent[:, : t * t])
+    right_c = matrix(sent[:, t * t :])
+    tri_c = jnp.einsum("ki,kj->ij", pick(left_c), right_c, preferred_element_type=jnp.float32)
+    tri_c = tri_c.astype(jnp.bfloat16).reshape(rows, half_t, cols, t).transpose(0, 2, 1, 3)
+    tri = exchange(tri_c.reshape(rows * cols, half_t * t))
+    triangle = (
+        tri.reshape(channels, 2 * half_t, t).transpose(1, 2, 0).astype(jnp.float32)
+    )
     tri_hat, tri_inv = normalize(triangle)
     onorm = (tri_hat * out_gain).astype(jnp.bfloat16)
     projected = jnp.einsum("ijc,cd->ijd", onorm, out_weight, preferred_element_type=jnp.float32)
@@ -57,20 +80,25 @@
     donorm = jnp.einsum("ijd,cd->ijc", dproj, out_weight, preferred_element_type=jnp.float32)
     out_gain_local = jnp.sum(donorm * tri_hat, axis=(0, 1))
     dtri = layer_back(donorm * out_gain, tri_hat, tri_inv).astype(jnp.bfloat16)
-    do_panels = lax.all_gather(dtri, "row", axis=0, tiled=True)
-    piece = do_panels
-    dleft = jnp.transpose(
-        lax.psum_scatter(
-            jnp.einsum("ijc,kjc->ikc", piece, right, preferred_element_type=jnp.float32).astype(
-                jnp.bfloat16
-            ),
-            "col",
-            scatter_dimension=0,
-            tiled=True,
-        ).astype(jnp.float32),
-        (1, 0, 2),
-    )
-    dright = jnp.einsum("kic,ijc->kjc", panels, do_panels, preferred_element_type=jnp.float32)
+    dtri_c = matrix(exchange(out_full(dtri)))
+    dtri_rows = lax.dynamic_index_in_dim(
+        dtri_c.reshape(rows, 2, half_t, cols * t), half, 1, keepdims=False
+    ).reshape(rows * half_t, cols * t)
+    dleft_c = jnp.einsum("kj,ij->ki", right_c, dtri_rows, preferred_element_type=jnp.float32)
+    dright_c = jnp.einsum("ki,ij->kj", left_c, pick(dtri_c), preferred_element_type=jnp.float32)
+
+    def back(x):
+        x = x.astype(jnp.bfloat16).reshape(rows, t, cols, half_t)
+        return x.transpose(0, 2, 1, 3).reshape(rows * cols, t * half_t)
+
+    grads = exchange(jnp.concatenate([back(dleft_c), back(dright_c)], axis=1))
+
+    def cells(x):
+        x = x.reshape(channels, 2, t, half_t).transpose(2, 1, 3, 0)
+        return x.reshape(t, t, channels).astype(jnp.float32)
+
+    dleft = cells(grads[:, : t * half_t])
+    dright = cells(grads[:, t * half_t :])
     dlin = jnp.concatenate(
         [
             dleft * mask_f * sig_left,

time: 760 us -> 660 us (0.87)
  waiting for transfers between devices: 582 us -> 306 us
  local copies, waits for them, and re-layouts: 40.6 us -> 154 us
  starting transfers between devices: 0.39 us -> 31.2 us
  other arithmetic: 18.9 us -> 40.9 us
  blocking collectives: 77 us -> 92.9 us
  matrix products: 26 us -> 14.6 us
    reduce_scatter x2 -> x0, waiting for transfers between devices: 174 us -> none  [the longest x1 95.7 us: body(): lax.psum_scatter(jnp.einsum('kic,kjc->ijc', piece, right, preferred_eleme...]
    all_gather x2 -> x0, waiting for transfers between devices: 162 us -> none  [the longest x1 98.2 us: body(): do_panels = lax.all_gather(dtri, 'row', axis=0, tiled=True)]
    all_to_all x0 -> x3, waiting for transfers between devices: none -> 61.1 us  [exchange(): return lax.all_to_all(x, AXES, split_axis=0, concat_axis=0, tiled=True)]
    reshape x0 -> x13, local copies, waits for them, and re-layouts: none -> 40.3 us  [the longest x5 17.7 us: matrix(): x.reshape(rows, cols, t, t).transpose(0, 2, 1, 3)]
    all_to_all x0 -> x3, starting transfers between devices: none -> 31.2 us  [exchange(): return lax.all_to_all(x, AXES, split_axis=0, concat_axis=0, tiled=True)]
    unnamed x24 -> x34, local copies, waits for them, and re-layouts: 1.81 us -> 31.1 us
    transpose x0 -> x7, local copies, waits for them, and re-layouts: none -> 26.2 us  [the longest x5 20.2 us: matrix(): x.reshape(rows, cols, t, t).transpose(0, 2, 1, 3)]
    all_to_all x0 -> x7, other arithmetic: none -> 23.7 us  [exchange(): return lax.all_to_all(x, AXES, split_axis=0, concat_axis=0, tiled=True)]
  transfers between devices with their start and end apart: 5 -> 4, of which waited for: 5 -> 4; matrix products, arithmetic and copies ran while one was open for 2% -> 2% of each run, Pallas kernels for 0% -> 0%
where the time goes in v1:
time: 660 us; the launch traced here: 653 us
  waiting for transfers between devices  306 us (46%)
  local copies, waits for them, and re-layouts  154 us (23%)
  blocking collectives  92.9 us (14%)
  other arithmetic  40.9 us (6%)
  starting transfers between devices  31.2 us (5%)
  matrix products  14.6 us (2%)
  between operations  14.6 us (2%)
    psum x1, waiting for transfers between devices, body(): lax.psum((proj_local, out_weight_local, in_gain_local, out_gain_local), (...  245 us
    psum x1, blocking collectives, body(): lax.psum((proj_local, out_weight_local, in_gain_local, out_gain_local), (...  72.4 us
    all_to_all x3, waiting for transfers between devices, exchange(): return lax.all_to_all(x, AXES, split_axis=0, concat_axis=0, tiled=True)  61.1 us
    all_to_all x3, starting transfers between devices, exchange(): return lax.all_to_all(x, AXES, split_axis=0, concat_axis=0, tiled=True)  31.2 us
    unnamed x34, local copies, waits for them, and re-layouts  31.1 us
    all_to_all x7, other arithmetic, exchange(): return lax.all_to_all(x, AXES, split_axis=0, concat_axis=0, tiled=True)  23.7 us
    all_to_all x1, blocking collectives, exchange(): return lax.all_to_all(x, AXES, split_axis=0, concat_axis=0, tiled=True)  20.4 us
    transpose x5, local copies, waits for them, and re-layouts, matrix(): x.reshape(rows, cols, t, t).transpose(0, 2, 1, 3)  20.2 us
  transfers between devices with their start and end apart: 4, of which 4 were waited for; matrix products, arithmetic and copies ran while one was open for 2% of the time, Pallas kernels for 0%

profile of v1, /device:TPU:1, one launch (start us, length us, event | category | flops | bytes accessed | tf_op | source)
XLA Modules:
  0.0 653.3 jit_solution(1382171473351890345)
XLA Ops:
  19.4 2.3 maximum_bitcast_fusion
  22.2 3.4 reduce.3
  25.6 2.6 reshape.165
  28.2 17.4 %all-to-all-start = ((bf16[256,2,1024]{2,1,0:T(2,128)(2,1)}), bf16[256,2,1024]{2,1,0:T(2,128)(2,1)}, u32[]{:S(2)}, u32[]{:S(2)}) async-start(bf16[256,2,1024]{2,1,0:T(2,128)(2,1)} %reshape.165), calls=%async_computation | async-start | bytes 2097152 | tf_op jit(solution)/shard_map/all_to_all | solution.py:25
  45.6 31.4 %all-to-all-done = bf16[256,2,1024]{2,1,0:T(2,128)(2,1)} async-done(((bf16[256,2,1024]{2,1,0:T(2,128)(2,1)}), bf16[256,2,1024]{2,1,0:T(2,128)(2,1)}, u32[]{:S(2)}, u32[]{:S(2)}) %all-to-all-start) | async-done | bytes 1048608 | tf_op jit(solution)/shard_map/all_to_all | solution.py:25
  77.0 7.5 %reshape.166 = bf16[256,1,2048]{2,1,0:T(2,128)(2,1)} reshape(bf16[256,2,1024]{2,1,0:T(2,128)(2,1)} %all-to-all-done) | data formatting | bytes 2097152
  84.5 2.2 copy.91
  87.5 2.6 reshape.140
  90.1 3.8 copy.68
  93.9 3.4 reshape.141
  97.3 3.9 reshape.142
  101.2 4.4 copy.69
  105.6 4.1 reshape_reshape.9
  111.7 2.5 reshape.144
  114.2 2.5 copy.92
  116.7 2.8 all_to_all.38
  119.4 2.9 reduce.4
  123.4 20.4 %all_to_all.44 = bf16[256,2,256]{2,1,0:T(2,128)(2,1)S(1)} all-to-all(bf16[256,2,256]{2,1,0:T(2,128)(2,1)S(1)} %reshape.167), channel_id=1, replica_groups=mesh['row'=16,'col'=16] {'row','col'}, dimensions={0} | all-to-all | bytes 524288 | tf_op jit(solution)/shard_map/all_to_all | solution.py:25
  144.7 2.5 convert_reduce_fusion.1
  147.3 1.8 reshape.155
  149.1 2.7 copy.73
  152.4 1.6 multiply_reduce_fusion
  155.3 1.8 copy.74
  157.2 2.0 broadcast_in_dim.17
  159.2 4.3 all_to_all.39
  163.5 5.6 reduce.5
  169.1 2.2 reshape.169
  171.3 7.0 %all-to-all-start.2 = ((bf16[256,2,512]{2,1,0:T(2,128)(2,1)}), bf16[256,2,512]{2,1,0:T(2,128)(2,1)}, u32[]{:S(2)}, u32[]{:S(2)}) async-start(bf16[256,2,512]{2,1,0:T(2,128)(2,1)} %reshape.169), calls=%async_computation.2 | async-start | bytes 1048576 | tf_op jit(solution)/shard_map/all_to_all | solution.py:25
  178.4 3.8 copy.79
  182.1 4.1 reshape.149
  186.2 12.2 %all-to-all-done.2 = bf16[256,2,512]{2,1,0:T(2,128)(2,1)} async-done(((bf16[256,2,512]{2,1,0:T(2,128)(2,1)}), bf16[256,2,512]{2,1,0:T(2,128)(2,1)}, u32[]{:S(2)}, u32[]{:S(2)}) %all-to-all-start.2) | async-done | bytes 524320 | tf_op jit(solution)/shard_map/all_to_all | solution.py:25
  198.5 4.4 reshape.170
  202.9 4.9 reduce.1
  207.8 3.7 reshape.145
  211.5 4.4 copy.80
  216.0 3.8 copy.76
  219.8 4.1 reshape_reshape.11
  224.8 2.1 convolution_convert_fusion
  226.9 1.8 copy.81
  228.7 4.1 reshape_reshape.10
  233.8 2.1 convolution_convert_fusion.1
  235.8 1.8 copy.77
  237.6 2.9 reshape.147
  240.5 2.5 reshape.151
  243.0 3.0 copy.82
  246.0 5.1 reshape.152
  251.1 3.0 copy.78
  254.1 5.1 reshape.148
  259.2 1.9 maximum_bitcast_fusion.1
  261.1 2.7 reduce.6
  263.8 2.2 reshape.171
  266.0 6.8 %all-to-all-start.3 = ((bf16[256,2,512]{2,1,0:T(2,128)(2,1)}), bf16[256,2,512]{2,1,0:T(2,128)(2,1)}, u32[]{:S(2)}, u32[]{:S(2)}) async-start(bf16[256,2,512]{2,1,0:T(2,128)(2,1)} %reshape.171), calls=%async_computation.3 | async-start | bytes 1048576 | tf_op jit(solution)/shard_map/all_to_all | solution.py:25
  272.9 2.2 convolution_bitcast_fusion.1
  275.0 17.4 %all-to-all-done.3 = bf16[256,2,512]{2,1,0:T(2,128)(2,1)} async-done(((bf16[256,2,512]{2,1,0:T(2,128)(2,1)}), bf16[256,2,512]{2,1,0:T(2,128)(2,1)}, u32[]{:S(2)}, u32[]{:S(2)}) %all-to-all-start.3) | async-done | bytes 524320 | tf_op jit(solution)/shard_map/all_to_all | solution.py:25
  292.4 4.6 reshape.172
  299.5 3.7 reshape.158
  303.2 4.5 copy.85
  307.7 3.7 reshape.157
  311.4 4.5 copy.84
  315.9 1.7 multiply_convert_fusion.1
  321.6 2.1 fusion.14
  323.7 72.4 %all-reduce = (f32[128]{0:T(128)S(1)}, f32[128]{0:T(128)S(1)}) all-reduce(f32[128]{0:T(128)S(1)} %get-tuple-element.7, f32[128]{0:T(128)S(1)} %get-tuple-element.5), channel_id=1, replica_groups=mesh['row'=16,'col'=16] {'row','col'}, use_global_device_ids=true, to_apply=%region_11.12 | all-reduce | flops 256 | bytes 2048 | tf_op jit(solution)/shard_map/psum | solution.py:116
  398.6 244.5 %all-reduce.4.cloned.1.call-done = (f32[128,640]{1,0:T(8,128)}, f32[128,128]{1,0:T(8,128)}) async-done(((f32[128,640]{1,0:T(8,128)}, f32[128,128]{1,0:T(8,128)}), (f32[128,640]{1,0:T(8,128)}, f32[128,128]{1,0:T(8,128)})) %all-reduce.4.cloned.1.call-update) | async-done | bytes 393232 | tf_op jit(solution)/shard_map/psum | solution.py:116
  643.1 1.7 broadcast_multiply_fusion
  (63 shorter events, 31.7 us)
Async XLA Ops:
  7.2 3.3 copy-start
  7.2 4.9 copy-start.5
  28.2 48.8 %all-to-all-start = ((bf16[256,2,1024]{2,1,0:T(2,128)(2,1)}), bf16[256,2,1024]{2,1,0:T(2,128)(2,1)}, u32[]{:S(2)}, u32[]{:S(2)}) async-start(bf16[256,2,1024]{2,1,0:T(2,128)(2,1)} %reshape.165), calls=%async_computation | async-start | bytes 2097152 | tf_op jit(solution)/shard_map/all_to_all | solution.py:25
  97.3 13.4 %copy-start.3 = (bf16[512,512]{1,0:T(8,128)(2,1)}, bf16[512,512]{1,0:T(8,128)(2,1)S(1)}, u32[]{:S(2)}) copy-start(bf16[512,512]{1,0:T(8,128)(2,1)S(1)} %reshape.141) | copy-start | bytes 1572868
  149.1 3.3 copy-start.7
  149.1 3.3 copy-start.9
  171.3 27.1 %all-to-all-start.2 = ((bf16[256,2,512]{2,1,0:T(2,128)(2,1)}), bf16[256,2,512]{2,1,0:T(2,128)(2,1)}, u32[]{:S(2)}, u32[]{:S(2)}) async-start(bf16[256,2,512]{2,1,0:T(2,128)(2,1)} %reshape.169), calls=%async_computation.2 | async-start | bytes 1048576 | tf_op jit(solution)/shard_map/all_to_all | solution.py:25
  266.0 26.4 %all-to-all-start.3 = ((bf16[256,2,512]{2,1,0:T(2,128)(2,1)}), bf16[256,2,512]{2,1,0:T(2,128)(2,1)}, u32[]{:S(2)}, u32[]{:S(2)}) async-start(bf16[256,2,512]{2,1,0:T(2,128)(2,1)} %reshape.171), calls=%async_computation.3 | async-start | bytes 1048576 | tf_op jit(solution)/shard_map/all_to_all | solution.py:25
  272.8 370.3 %all-reduce.4.cloned.1.call-start = ((), (), s32[]{:S(2)}) async-start(), calls=%async_computation.4 | async-start | bytes 786432 | tf_op jit(solution)/shard_map/psum | solution.py:116
  317.6 1.0 copy-start.6
  317.8 2.3 copy-start.1
  317.8 2.3 copy-start.8
  319.0 1.1 copy-start.4
  320.1 76.6 %copy-start.2 = (bf16[32,32,128]{2,1,0:T(8,128)(2,1)S(1)}, bf16[32,32,128]{2,1,0:T(8,128)(2,1)}, u32[]{:S(2)}) copy-start(bf16[32,32,128]{2,1,0:T(8,128)(2,1)} %param.7) | copy-start | bytes 786436
Sparse Core Ops, SparseCore 0:
  396.8 246.3 all-reduce.3

commit v2 on v0

v2 whole, which is shorter than its diff:
```python
import jax
import jax.numpy as jnp
from jax import lax
from jax.experimental import pallas as pl
from jax.experimental.pallas import tpu as pltpu
from jax.sharding import PartitionSpec as P


def normalize(values):
    average = jnp.mean(values, axis=-1, keepdims=True)
    centred = values - average
    spread = jnp.mean(centred * centred, axis=-1, keepdims=True)
    inverse = lax.rsqrt(spread + 1e-05)
    return (centred * inverse, inverse)


def layer_back(grad_hat, normed, inverse):
    first_mean = jnp.mean(grad_hat, axis=-1, keepdims=True)
    second_mean = jnp.mean(grad_hat * normed, axis=-1, keepdims=True)
    return (grad_hat - first_mean - normed * second_mean) * inverse


MESH = pl.DeviceIdType.MESH


def settle(ref, sem):
    pltpu.make_async_copy(ref, ref, sem).wait()


def place():
    row = lax.axis_index("row")
    col = lax.axis_index("col")
    return row, col, row * 8 + col // 2, lax.rem(col, 2)


def chip_peer(chip, core):
    return (chip // 8, lax.rem(chip, 8) * 2 + core)


def cell_peer(cell, core):
    return (core * 8 + cell // 16, lax.rem(cell, 16))


def greet(peers, count, own):
    barrier = pltpu.get_barrier_semaphore()

    def step(s, carry):
        row, col, mine = peers(s)

        @pl.when(mine == 0)
        def _():
            pl.semaphore_signal(barrier, inc=1, device_id=(row, col), device_id_type=MESH)

        return carry

    lax.fori_loop(0, count, step, 0)
    pl.semaphore_wait(barrier, count - own)


def spread(x_ref, o_ref, send_sem, recv_sem, to_chip):
    row, col, chip, core = place()
    half = row // 8
    own = 1 - lax.rem(half + core, 2)
    cell = lax.rem(row, 8) * 16 + col
    start, slot = (chip, cell) if to_chip else (cell, chip)

    def is_mine(t, base):
        return jnp.where(t == base, own, 0)

    def toward_chip(s):
        t = lax.rem(chip + s, 128)
        return (*chip_peer(t, half), is_mine(t, chip))

    def toward_cell(s):
        t = lax.rem(cell + s, 128)
        return (*cell_peer(t, core), is_mine(t, cell))

    goes, comes = (toward_chip, toward_cell) if to_chip else (toward_cell, toward_chip)
    greet(comes, 128, own)

    def step(s, carry):
        block = lax.rem(start + s, 128)
        to_row, to_col, mine = goes(s)

        @pl.when(mine == 0)
        def _():
            pltpu.make_async_remote_copy(
                x_ref.at[block],
                o_ref.at[slot],
                send_sem,
                recv_sem,
                device_id=(to_row, to_col),
                device_id_type=MESH,
            ).start()

        @pl.when(mine == 1)
        def _():
            pltpu.make_async_copy(x_ref.at[block], o_ref.at[slot], recv_sem).start()

        return carry

    lax.fori_loop(0, 128, step, 0)
    settle(o_ref, recv_sem)
    settle(x_ref.at[pl.ds(0, 127)], send_sem)

    @pl.when(own == 0)
    def _():
        settle(x_ref.at[0], send_sem)


def transport(x, to_chip, number):
    def kernel(x_ref, o_ref, send_sem, recv_sem):
        spread(x_ref, o_ref, send_sem, recv_sem, to_chip)

    return pl.pallas_call(
        kernel,
        out_shape=jax.ShapeDtypeStruct(x.shape, x.dtype),
        in_specs=[pl.BlockSpec(memory_space=pltpu.VMEM)],
        out_specs=pl.BlockSpec(memory_space=pltpu.VMEM),
        scratch_shapes=[pltpu.SemaphoreType.DMA(()), pltpu.SemaphoreType.DMA(())],
        name=f"transport{number}",
        compiler_params=pltpu.CompilerParams(collective_id=number, has_side_effects=True),
    )(x)


def sum_kernel(x_ref, o_ref, held, send_sem, recv_sem, send_sem2, recv_sem2):
    row, col, _, _ = place()
    me = row * 16 + col
    barrier = pltpu.get_barrier_semaphore()

    def peer(s):
        d = lax.rem(me + s, 256)
        return d, (d // 16, lax.rem(d, 16))

    def hello(s, carry):
        pl.semaphore_signal(barrier, inc=1, device_id=peer(s)[1], device_id_type=MESH)
        return carry

    lax.fori_loop(1, 256, hello, 0)
    pl.semaphore_wait(barrier, 255)

    def scatter(s, carry):
        d, where = peer(s)
        pltpu.make_async_remote_copy(
            x_ref.at[d], held.at[me], send_sem, recv_sem, device_id=where, device_id_type=MESH
        ).start()
        return carry

    pltpu.make_async_copy(x_ref.at[me], held.at[me], recv_sem).start()
    lax.fori_loop(1, 256, scatter, 0)
    settle(held, recv_sem)
    o_ref[me] = jnp.sum(held[...], axis=0)

    def gather(s, carry):
        pltpu.make_async_remote_copy(
            o_ref.at[me], o_ref.at[me], send_sem2, recv_sem2, device_id=peer(s)[1], device_id_type=MESH
        ).start()
        return carry

    lax.fori_loop(1, 256, gather, 0)
    rest = o_ref.at[pl.ds(0, 255)]
    settle(rest, recv_sem2)
    settle(rest, send_sem)
    settle(rest, send_sem2)


def sum_all(x):
    return pl.pallas_call(
        sum_kernel,
        out_shape=jax.ShapeDtypeStruct(x.shape, x.dtype),
        in_specs=[pl.BlockSpec(memory_space=pltpu.VMEM)],
        out_specs=pl.BlockSpec(memory_space=pltpu.VMEM),
        scratch_shapes=[pltpu.VMEM(x.shape, x.dtype)] + [pltpu.SemaphoreType.DMA(())] * 4,
        name="sum_all",
        compiler_params=pltpu.CompilerParams(collective_id=5, has_side_effects=True),
    )(x)


def body(pair, pair_mask, proj_weight, out_weight, in_gain, out_gain, cotangent):
    t = pair.shape[0]
    channels = pair.shape[2]
    rows = lax.axis_size("row")
    cols = lax.axis_size("col")
    total = t * rows
    core = lax.rem(lax.axis_index("col"), 2)
    halves = rows // 2
    partner = [(k, k + 1 - 2 * (k % 2)) for k in range(cols)]
    normed, inverse = normalize(pair.astype(jnp.float32))
    zn = (normed * in_gain).astype(jnp.bfloat16)
    linear = jnp.einsum("ijc,ce->ije", zn, proj_weight, preferred_element_type=jnp.float32)
    proj_left = linear[..., 0:channels]
    gate_left = linear[..., channels : 2 * channels]
    proj_right = linear[..., 2 * channels : 3 * channels]
    gate_right = linear[..., 3 * channels : 4 * channels]
    gate_out = linear[..., 4 * channels :]
    mask_f = pair_mask.astype(jnp.float32)[..., None]
    sig_left = jax.nn.sigmoid(gate_left)
    sig_right = jax.nn.sigmoid(gate_right)
    left = (mask_f * sig_left * proj_left).astype(jnp.bfloat16)
    right = (mask_f * sig_right * proj_right).astype(jnp.bfloat16)

    def by_channel(x):
        return jnp.transpose(x, (2, 0, 1)).reshape(channels, 1, 8, 128)

    def matrix(x):
        x = x.reshape(halves, cols, t, t).transpose(0, 2, 1, 3)
        return x.reshape(halves * t, cols * t)

    def blocks(x):
        x = x.reshape(halves, t, cols, t).transpose(0, 2, 1, 3)
        return x.reshape(halves * cols, 1, 8, 128)

    def to_other(x):
        return lax.ppermute(x, "col", partner)

    def pick(x, index):
        return lax.dynamic_index_in_dim(x.reshape(2, halves * t, cols * t), index, 0, keepdims=False)

    def cells(x):
        return x.reshape(channels, t, t).transpose(1, 2, 0).astype(jnp.float32)

    sent = transport(jnp.concatenate([by_channel(left), by_channel(right)], axis=1), True, 0)
    left_c = matrix(sent[:, 0])
    right_c = matrix(sent[:, 1])
    part = jnp.einsum("ki,kj->ij", left_c, right_c, preferred_element_type=jnp.float32)
    other = to_other(pick(part, 1 - core).astype(jnp.bfloat16)).astype(jnp.float32)
    tri_c = (pick(part, core) + other).astype(jnp.bfloat16)
    triangle = cells(transport(blocks(tri_c), False, 1)[:, 0])
    tri_hat, tri_inv = normalize(triangle)
    onorm = (tri_hat * out_gain).astype(jnp.bfloat16)
    projected = jnp.einsum("ijc,cd->ijd", onorm, out_weight, preferred_element_type=jnp.float32)
    sig_gate = jax.nn.sigmoid(gate_out)
    cot_f = cotangent.astype(jnp.float32)
    dproj = (cot_f * sig_gate).astype(jnp.bfloat16)
    dgate = cot_f * projected * sig_gate * (1.0 - sig_gate)
    out_weight_local = jnp.einsum("ijc,ijd->cd", onorm, dproj, preferred_element_type=jnp.float32)
    donorm = jnp.einsum("ijd,cd->ijc", dproj, out_weight, preferred_element_type=jnp.float32)
    dtri = layer_back(donorm * out_gain, tri_hat, tri_inv).astype(jnp.bfloat16)
    dtri_half = matrix(transport(by_channel(dtri), True, 2)[:, 0])
    dtri_other = to_other(dtri_half)
    dtri_c = jnp.where(
        core == 0,
        jnp.concatenate([dtri_half, dtri_other], axis=0),
        jnp.concatenate([dtri_other, dtri_half], axis=0),
    )
    dleft_c = jnp.einsum("kj,ij->ki", right_c, dtri_c, preferred_element_type=jnp.float32)
    dright_c = jnp.einsum("ki,ij->kj", left_c, dtri_c, preferred_element_type=jnp.float32)
    grads = jnp.concatenate(
        [blocks(dleft_c.astype(jnp.bfloat16)), blocks(dright_c.astype(jnp.bfloat16))], axis=1
    )
    grads = transport(grads, False, 3)
    dleft = cells(grads[:, 0])
    dright = cells(grads[:, 1])
    dlin = jnp.concatenate(
        [
            dleft * mask_f * sig_left,
            dleft * mask_f * proj_left * sig_left * (1.0 - sig_left),
            dright * mask_f * sig_right,
            dright * mask_f * proj_right * sig_right * (1.0 - sig_right),
            dgate,
        ],
        axis=-1,
    ).astype(jnp.bfloat16)
    proj_local = jnp.einsum("ijc,ije->ce", zn, dlin, preferred_element_type=jnp.float32)
    dzn = jnp.einsum("ije,ce->ijc", dlin, proj_weight, preferred_element_type=jnp.float32)
    d_pair = layer_back(dzn * in_gain, normed, inverse)
    sums = sum_all(
        jnp.concatenate([proj_local.reshape(-1, 128), out_weight_local], axis=0).reshape(-1, 3, 128)
    ).reshape(-1, 128)
    scale = 1.0 / total
    d_proj = sums[: channels * 5].reshape(channels, 5 * channels) * scale
    d_out = sums[channels * 5 :] * scale
    d_in_gain = jnp.sum(d_proj * proj_weight.astype(jnp.float32), axis=1) / in_gain
    d_out_gain = jnp.sum(d_out * out_weight.astype(jnp.float32), axis=1) / out_gain
    return (d_pair, d_proj, d_out, d_in_gain, d_out_gain)


def solution(mesh):
    in_specs = (P("row", "col", None), P("row", "col"), P(), P(), P(), P(), P("row", "col", None))
    out_specs = (P("row", "col", None), P(), P(), P(), P())
    return jax.shard_map(body, mesh=mesh, in_specs=in_specs, out_specs=out_specs, check_vma=False)
```

time: 760 us -> 232 us (0.31)
  waiting for transfers between devices: 582 us -> 1.3 us
  Pallas kernels: 0 us -> 138 us
  blocking collectives: 77 us -> 0 us
  local copies, waits for them, and re-layouts: 40.6 us -> 58.8 us
  matrix products: 26 us -> 10.7 us
  between operations: 14 us -> 1 us
    psum x1 -> x0, waiting for transfers between devices: 246 us -> none  [body(): lax.psum((proj_local, out_weight_local, in_gain_local, out_gain_local), (...]
    reduce_scatter x2 -> x0, waiting for transfers between devices: 174 us -> none  [the longest x1 95.7 us: body(): lax.psum_scatter(jnp.einsum('kic,kjc->ijc', piece, right, preferred_eleme...]
    all_gather x2 -> x0, waiting for transfers between devices: 162 us -> none  [the longest x1 98.2 us: body(): do_panels = lax.all_gather(dtri, 'row', axis=0, tiled=True)]
    pallas_call x0 -> x5, Pallas kernels: none -> 138 us  [the longest x4 90.6 us: transport(): pl.pallas_call(kernel, out_shape=jax.ShapeDtypeStruct(x.shape, x.dtype),...]
    psum x1 -> x0, blocking collectives: 77 us -> none  [body(): lax.psum((proj_local, out_weight_local, in_gain_local, out_gain_local), (...]
    reshape x0 -> x19, local copies, waits for them, and re-layouts: none -> 36.1 us  [the longest x6 13.3 us: blocks(): x = x.reshape(halves, t, cols, t).transpose(0, 2, 1, 3)]
    dot_general x3 -> x1, local copies, waits for them, and re-layouts: 19.9 us -> 0.84 us  [body(): jnp.einsum('ki,kj->ij', left_c, right_c, preferred_element_type=jnp.float32)]
    all_gather x2 -> x0, local copies, waits for them, and re-layouts: 16.6 us -> none  [the longest x1 8.6 us: body(): do_panels = lax.all_gather(dtri, 'row', axis=0, tiled=True)]
  transfers between devices with their start and end apart: 5 -> 2, of which waited for: 5 -> 1; matrix products, arithmetic and copies ran while one was open for 2% -> 2% of each run, Pallas kernels for 0% -> 0%
where the time goes in v2:
time: 232 us; the launch traced here: 230 us
  Pallas kernels  138 us (59%)
  local copies, waits for them, and re-layouts  58.8 us (25%)
  other arithmetic  18 us (8%)
  matrix products  10.7 us (5%)
  starting transfers between devices  2.48 us (1%)
    pallas_call x4, Pallas kernels, transport(): pl.pallas_call(kernel, out_shape=jax.ShapeDtypeStruct(x.shape, x.dtype),...  90.6 us
    pallas_call x1, Pallas kernels, sum_all(): pl.pallas_call(sum_kernel, out_shape=jax.ShapeDtypeStruct(x.shape, x.dtyp...  47.3 us
    reshape x6, local copies, waits for them, and re-layouts, blocks(): x = x.reshape(halves, t, cols, t).transpose(0, 2, 1, 3)  13.3 us
    another operation x5, local copies, waits for them, and re-layouts, matrix(): x = x.reshape(halves, cols, t, t).transpose(0, 2, 1, 3)  10.6 us
    reshape x4, local copies, waits for them, and re-layouts, matrix(): return x.reshape(halves * t, cols * t)  10.1 us
    reshape x3, local copies, waits for them, and re-layouts, blocks(): return x.reshape(halves * cols, 1, 8, 128)  7.62 us
    convert_element_type x3, local copies, waits for them, and re-layouts, cells(): return x.reshape(channels, t, t).transpose(1, 2, 0).astype(jnp.float32)  5.26 us
  transfers between devices with their start and end apart: 2, of which 1 were waited for; matrix products, arithmetic and copies ran while one was open for 2% of the time, Pallas kernels for 0%

profile of v2, /device:TPU:1, one launch (start us, length us, event | category | flops | bytes accessed | tf_op | source)
XLA Modules:
  0.0 230.2 jit_solution(4100811501644239048)
XLA Ops:
  0.6 0.7 convert_element_type.80
  1.4 1.2 convert_reduce_fusion
  2.5 1.3 fusion.13
  3.9 1.7 fusion.41
  5.6 0.5 multiply_convert_fusion.2
  6.0 0.9 copy.23
  7.1 1.8 pad_maximum_fusion.x_ref
  8.9 30.7 %transport0.1 = bf16[128,2,8,128]{3,2,1,0:T(8,128)(2,1)} custom-call(bf16[128,2,8,128]{3,2,1,0:T(8,128)(2,1)} %pad_maximum_fusion.x_ref), custom_call_target="tpu_custom_call" | custom-call | tf_op jit(solution)/shard_map/transport0/pallas_call | solution.py:115
  39.7 1.1 fusion.51
  40.8 1.4 reshape_squeeze.12
  42.2 2.6 %copy.25 = bf16[8,32,16,32]{3,2,1,0:T(8,128)(2,1)} copy(bf16[8,32,16,32]{3,1,2,0:T(8,128)(2,1)} %bitcast.128) | data formatting | bytes 524288 | tf_op jit(solution)/shard_map/transpose | solution.py:206
  44.8 2.2 reshape.134
  47.0 1.4 reshape_squeeze.13
  48.5 2.6 %copy.45 = bf16[8,16,32,32]{3,1,2,0:T(8,128)(2,1)} copy(bf16[8,16,32,32]{3,2,1,0:T(8,128)(2,1)} %reshape_squeeze.13) | data formatting | bytes 524288 | tf_op jit(solution)/shard_map/reshape;squeeze | solution.py:206
  51.1 2.2 reshape.116
  53.3 0.8 copy.27
  54.2 1.2 fusion.52
  55.4 1.0 copy-done.3
  56.5 2.5 %collective-permute-start = (bf16[256,512]{1,0:T(8,128)(2,1)S(1)}, bf16[256,512]{1,0:T(8,128)(2,1)}, u32[]{:S(2)}, u32[]{:S(2)}) collective-permute-start(bf16[256,512]{1,0:T(8,128)(2,1)S(1)} %fusion.35), channel_id=1, source_target_pairs={{0,1},{1,0},{2,3},{3,2},{4,5},{5,4},{6,7},{7,6},{8,9},{9,8},{10,11... | collective-permute-start | bytes 786440 | tf_op jit(solution)/shard_map/ppermute | solution.py:214
  59.0 1.3 collective-permute-done
  60.3 1.2 fusion.32
  61.5 1.6 reshape.117
  63.1 2.5 %copy.44 = bf16[8,32,16,32]{3,1,2,0:T(8,128)(2,1)} copy(bf16[8,32,16,32]{3,2,1,0:T(8,128)(2,1)} %reshape.117) | data formatting | bytes 524288 | tf_op jit(solution)/shard_map/reshape | solution.py:210
  65.6 2.5 %reshape.118.x_ref = bf16[128,1,8,128]{3,2,1,0:T(8,128)(2,1)} reshape(bf16[8,16,32,32]{3,2,1,0:T(8,128)(2,1)} %bitcast.130) | data formatting | bytes 524288 | tf_op jit(solution)/shard_map/reshape | solution.py:211
  68.1 19.0 %transport1.1 = bf16[128,1,8,128]{3,2,1,0:T(8,128)(2,1)} custom-call(bf16[128,1,8,128]{3,2,1,0:T(8,128)(2,1)} %reshape.118.x_ref), custom_call_target="tpu_custom_call" | custom-call | tf_op jit(solution)/shard_map/transport1/pallas_call | solution.py:115
  87.1 1.2 copy.29
  88.5 0.4 multiply_reduce_fusion.1
  88.9 0.8 fusion.50
  89.8 1.3 fusion.34
  91.1 1.8 copy.30.x_ref
  92.9 21.7 %transport2.1 = bf16[128,1,8,128]{3,2,1,0:T(8,128)(2,1)} custom-call(bf16[128,1,8,128]{3,2,1,0:T(8,128)(2,1)} %copy.30.x_ref), custom_call_target="tpu_custom_call" | custom-call | tf_op jit(solution)/shard_map/transport2/pallas_call | solution.py:115
  114.7 2.5 %reshape_squeeze.14 = bf16[8,16,32,32]{3,2,1,0:T(8,128)(2,1)} reshape(bf16[128,1,8,128]{3,2,1,0:T(8,128)(2,1)} %transport2.1) | data formatting | bytes 524288 | tf_op jit(solution)/shard_map/reshape;squeeze | solution.py:206
  117.2 2.6 %copy.43 = bf16[8,16,32,32]{3,1,2,0:T(8,128)(2,1)} copy(bf16[8,16,32,32]{3,2,1,0:T(8,128)(2,1)} %reshape_squeeze.14) | data formatting | bytes 524288 | tf_op jit(solution)/shard_map/reshape;squeeze | solution.py:206
  119.8 2.8 %reshape.120 = bf16[256,512]{1,0:T(8,128)(2,1)} reshape(bf16[8,32,16,32]{3,2,1,0:T(8,128)(2,1)} %bitcast.131) | data formatting | bytes 524288 | tf_op jit(solution)/shard_map/reshape | solution.py:207
  122.6 2.8 %reshape.115 = bf16[256,512]{1,0:T(8,128)(2,1)} reshape(bf16[8,32,16,32]{3,2,1,0:T(8,128)(2,1)} %copy.25) | data formatting | bytes 524288 | tf_op jit(solution)/shard_map/reshape | solution.py:207
  125.4 1.2 convolution_bitcast_fusion.1
  126.7 1.6 convolution_convert_fusion.1
  128.3 1.6 reshape.121
  129.9 2.5 %copy.42 = bf16[8,32,16,32]{3,1,2,0:T(8,128)(2,1)} copy(bf16[8,32,16,32]{3,2,1,0:T(8,128)(2,1)} %reshape.121) | data formatting | bytes 524288 | tf_op jit(solution)/shard_map/reshape | solution.py:210
  132.4 2.5 %reshape.122 = bf16[128,1,8,128]{3,2,1,0:T(8,128)(2,1)} reshape(bf16[8,16,32,32]{3,2,1,0:T(8,128)(2,1)} %bitcast.132) | data formatting | bytes 524288 | tf_op jit(solution)/shard_map/reshape | solution.py:211
  135.0 2.2 convolution_convert_fusion
  137.2 2.5 %reshape.123 = bf16[8,32,16,32]{3,2,1,0:T(8,128)(2,1)} reshape(bf16[256,512]{1,0:T(8,128)(2,1)} %convolution_convert_fusion) | data formatting | bytes 524288 | tf_op jit(solution)/shard_map/reshape | solution.py:210
  139.7 2.6 %copy.41 = bf16[8,32,16,32]{3,1,2,0:T(8,128)(2,1)} copy(bf16[8,32,16,32]{3,2,1,0:T(8,128)(2,1)} %reshape.123) | data formatting | bytes 524288 | tf_op jit(solution)/shard_map/reshape | solution.py:210
  142.3 2.5 %reshape.124 = bf16[128,1,8,128]{3,2,1,0:T(8,128)(2,1)} reshape(bf16[8,16,32,32]{3,2,1,0:T(8,128)(2,1)} %bitcast.133) | data formatting | bytes 524288 | tf_op jit(solution)/shard_map/reshape | solution.py:211
  144.8 1.8 pad_maximum_fusion.1.x_ref
  146.6 19.1 %transport3.1 = bf16[128,2,8,128]{3,2,1,0:T(8,128)(2,1)} custom-call(bf16[128,2,8,128]{3,2,1,0:T(8,128)(2,1)} %pad_maximum_fusion.1.x_ref), custom_call_target="tpu_custom_call" | custom-call | tf_op jit(solution)/shard_map/transport3/pallas_call | solution.py:115
  165.7 2.1 slice_convert_fusion
  167.8 2.1 copy.35
  169.9 2.0 copy.34
  171.9 1.3 fusion.37
  173.2 0.3 fusion.36
  173.8 0.3 fusion.38
  174.1 0.4 copy-done.10
  174.5 0.5 fusion.3
  175.0 0.4 copy-done
  175.5 0.8 convolution_bitcast_fusion
  176.4 0.7 fusion.49
  177.2 1.0 reshape.126.x_ref
  178.2 47.3 %sum_all.1 = f32[256,3,128]{2,1,0:T(4,128)} custom-call(f32[256,3,128]{2,1,0:T(4,128)} %reshape.126.x_ref), custom_call_target="tpu_custom_call" | custom-call | tf_op jit(solution)/shard_map/sum_all/pallas_call | solution.py:168
  225.5 1.2 reshape.127
  226.8 0.6 multiply_reduce_fusion.3
  227.5 0.6 div.51
  228.2 0.5 div.50
  228.7 1.4 fusion.12
  (45 shorter events, 1.3 us)
Async XLA Ops:
  3.9 1.7 copy-start.9
  53.3 3.2 %copy-start.5 = (bf16[256,512]{1,0:T(8,128)(2,1)}, bf16[256,512]{1,0:T(8,128)(2,1)S(1)}, u32[]{:S(2)}) copy-start(bf16[256,512]{1,0:T(8,128)(2,1)S(1)} %reshape.116) | copy-start | bytes 786436
  55.4 1.0 copy-start.3
  56.5 3.8 %collective-permute-start = (bf16[256,512]{1,0:T(8,128)(2,1)S(1)}, bf16[256,512]{1,0:T(8,128)(2,1)}, u32[]{:S(2)}, u32[]{:S(2)}) collective-permute-start(bf16[256,512]{1,0:T(8,128)(2,1)S(1)} %fusion.35), channel_id=1, source_target_pairs={{0,1},{1,0},{2,3},{3,2},{4,5},{5,4},{6,7},{7,6},{8,9},{9,8},{10,11... | collective-permute-start | bytes 786440 | tf_op jit(solution)/shard_map/ppermute | solution.py:214
  68.1 20.8 %copy-start.11 = (bf16[128,128]{1,0:T(8,128)(2,1)S(1)}, bf16[128,128]{1,0:T(8,128)(2,1)}, u32[]{:S(2)}) copy-start(bf16[128,128]{1,0:T(8,128)(2,1)} %param.10) | copy-start | bytes 98308
  68.1 20.8 %copy-start.14 = (f32[128]{0:T(128)S(1)}, f32[128]{0:T(128)}, u32[]{:S(2)}) copy-start(f32[128]{0:T(128)} %param.12) | copy-start | bytes 1540
  122.6 4.1 %collective-permute-start.1 = (bf16[256,512]{1,0:T(8,128)(2,1)}, bf16[256,512]{1,0:T(8,128)(2,1)}, u32[]{:S(2)}, u32[]{:S(2)}) collective-permute-start(bf16[256,512]{1,0:T(8,128)(2,1)} %reshape.120), channel_id=1, source_target_pairs={{0,1},{1,0},{2,3},{3,2},{4,5},{5,4},{6,7},{7,6},{8,9},{9,8},{10,11... | collective-permute-start | bytes 786440 | tf_op jit(solution)/shard_map/ppermute | solution.py:214
  129.9 5.1 %copy-start.6 = (bf16[256,512]{1,0:T(8,128)(2,1)S(1)}, bf16[256,512]{1,0:T(8,128)(2,1)}, u32[]{:S(2)}) copy-start(bf16[256,512]{1,0:T(8,128)(2,1)} %copy-done.5) | copy-start | bytes 786436
  139.7 5.1 %copy-start.7 = (bf16[128,1,8,128]{3,2,1,0:T(8,128)(2,1)S(1)}, bf16[128,1,8,128]{3,2,1,0:T(8,128)(2,1)}, u32[]{:S(2)}) copy-start(bf16[128,1,8,128]{3,2,1,0:T(8,128)(2,1)} %reshape.122) | copy-start | bytes 786436
  171.9 1.3 copy-start.2
  171.9 1.6 copy-start.1
  173.5 1.0 copy-start.10
  174.5 0.9 copy-start
  174.5 1.0 copy-start.13
  175.5 0.9 copy-start.8
  176.4 0.8 copy-start.12
  227.5 2.6 %copy-start.4 = (f32[128,640]{1,0:T(8,128)}, f32[128,640]{1,0:T(8,128)S(1)}, u32[]{:S(2)}) copy-start(f32[128,640]{1,0:T(8,128)S(1)} %mul.244) | copy-start | bytes 983044

commit v3 on v0

v3 whole, which is shorter than its diff:
```python
import jax
import jax.numpy as jnp
from jax import lax
from jax.experimental import pallas as pl
from jax.experimental.pallas import tpu as pltpu
from jax.sharding import PartitionSpec as P

MESH = pl.DeviceIdType.MESH
F32 = jnp.float32
BF16 = jnp.bfloat16
EPS = 1e-05


def settle(ref, sem):
    pltpu.make_async_copy(ref, ref, sem).wait()


def device(number):
    return (number // 16, lax.rem(number, 16))


def wrap(value, size):
    return jnp.where(value >= size, value - size, value)


def dot(a, b):
    return jnp.dot(a, b, preferred_element_type=F32)


def dot_nt(a, b):
    return lax.dot_general(a, b, (((1,), (1,)), ((), ())), preferred_element_type=F32)


def dot_tn(a, b):
    return lax.dot_general(a, b, (((0,), (0,)), ((), ())), preferred_element_type=F32)


def mean0(x):
    return jnp.sum(x, axis=0, keepdims=True) * (1.0 / x.shape[0])


def normalize(x):
    centred = x - mean0(x)
    inverse = lax.rsqrt(mean0(centred * centred) + EPS)
    return centred * inverse, inverse


def sigmoid(x):
    return 1.0 / (1.0 + jnp.exp(-x))


def send(src, dst, send_sem, recv_sem, number, me):
    @pl.when(number != me)
    def _():
        pltpu.make_async_remote_copy(
            src, dst, send_sem, recv_sem, device_id=device(number), device_id_type=MESH
        ).start()

    @pl.when(number == me)
    def _():
        pltpu.make_async_copy(src, dst, recv_sem).start()


def kernel(
    pair, mask, w_in, w_out, gain_in, gain_out, cot,
    d_pair, d_w_in, d_w_out, d_gain_in, d_gain_out,
    s1, r1, s2, r2, s3, r3, s4, r4,
    lane_swap, cell_mask, w_in_t, w_out_t, gi, go,
    zhat, s_z, zn, left, right, a_left, b_left, a_right, b_right, gate,
    dproj, upper, h, h_mean, m_left, m_right, part, part_out, part_in,
    tri, onorm, dtri, dtri_f, dtri_all, grad_l, grad_r, dlin,
    g_early, h_early, o_early, a_early, g_late, h_late, o_late, a_late,
    sems,
):
    row = lax.axis_index("row")
    col = lax.axis_index("col")
    me = row * 16 + col
    chip = row * 8 + col // 2
    core = lax.rem(col, 2)
    half = row // 8
    row8 = lax.rem(row, 8)
    cell = row8 * 16 + col
    partner = me + 1 - 2 * core
    own = 1 - lax.rem(half + core, 2)
    scale = 1.0 / 512.0

    barrier = pltpu.get_barrier_semaphore()

    def hello(s, carry):
        pl.semaphore_signal(
            barrier, inc=1, device_id=device(wrap(me + s, 256)), device_id_type=MESH
        )
        return carry

    lax.fori_loop(1, 256, hello, 0)

    def iota(shape, axis):
        return lax.broadcasted_iota(jnp.int32, shape, axis)

    r_i, c_i = iota((128, 128), 0), iota((128, 128), 1)
    to_block = jnp.where(c_i == (r_i & 7) * 16 + (r_i >> 3), 1.0, 0.0).astype(BF16)
    to_tiles = jnp.where(c_i == (r_i & 15) * 8 + (r_i >> 4), 1.0, 0.0).astype(BF16)

    w_in_t[...] = w_in[...].astype(F32).T.astype(BF16)
    w_out_t[...] = w_out[...].astype(F32).T.astype(BF16)
    gi[...] = jnp.broadcast_to(gain_in[...], (128, 128)).T
    go[...] = jnp.broadcast_to(gain_out[...], (128, 128)).T
    spread = jnp.where(iota((32, 128), 0) == (iota((32, 128), 1) & 31), 1.0, 0.0).astype(BF16)
    wide = dot(mask[...].astype(F32).astype(BF16), spread)
    wide = jnp.where((iota((32, 128), 0) >> 3) == (iota((32, 128), 1) >> 5), wide, 0.0)
    wide = wide[0:8] + wide[8:16] + wide[16:24] + wide[24:32]
    for j in range(8):
        cell_mask[j] = wide[j : j + 1]

    def tile(j):
        return pl.ds(pl.multiple_of(j * 128, 128), 128)

    def cells_in(ref, j):
        rows = jnp.concatenate([ref[8 * k + j] for k in range(4)], axis=0)
        return rows.astype(F32).T

    def project(j, carry):
        normed, inverse = normalize(cells_in(pair, j))
        zhat[j] = normed
        s_z[j] = inverse
        z = (normed * gi[...]).astype(BF16)
        zn[:, tile(j)] = z
        keep = cell_mask[j]
        lin = dot(w_in_t[0:256], z)
        sig = sigmoid(lin[128:256])
        value = keep * sig
        product = value * lin[0:128]
        left[j] = product.astype(BF16)
        a_left[j] = value
        b_left[j] = product * (1.0 - sig)
        lin = dot(w_in_t[256:512], z)
        sig = sigmoid(lin[128:256])
        value = keep * sig
        product = value * lin[0:128]
        right[j] = product.astype(BF16)
        a_right[j] = value
        b_right[j] = product * (1.0 - sig)
        return carry

    lax.fori_loop(0, 8, project, 0, unroll=2)

    def to_blocks(src, g):
        return dot(to_block, src[:, 16 * g : 16 * g + 16, :].reshape(128, 128)).reshape(
            16, 8, 128
        ).astype(BF16)

    for g in range(8):
        s1[16 * g : 16 * g + 16, 0] = to_blocks(left, g)
        s1[16 * g : 16 * g + 16, 1] = to_blocks(right, g)

    pl.semaphore_wait(barrier, 255)

    def to_chips(src, dst, k):
        def step(s, carry):
            c = wrap(chip + s, 128)
            send(src.at[c], dst.at[row8, col], sems.at[k], sems.at[k + 1], 2 * c + half, me)
            return carry

        lax.fori_loop(0, 128, step, 0)

    def to_cells(src, dst, k):
        def step(s, carry):
            t = wrap(cell + s, 128)
            send(
                src.at[t // 16, lax.rem(t, 16)], dst.at[chip], sems.at[k], sems.at[k + 1],
                core * 128 + t, me,
            )
            return carry

        lax.fori_loop(0, 128, step, 0)

    def sent(ref, k):
        settle(ref.at[pl.ds(0, 127)], sems.at[k])

        @pl.when(own == 0)
        def _():
            settle(ref.at[0], sems.at[k])

    to_chips(s1, r1, 0)

    l_i, l_o = iota((512, 512), 0), iota((512, 512), 1)
    lane_swap[...] = jnp.where(
        l_o == ((l_i & 96) << 2) + ((l_i >> 7) << 5) + (l_i & 31), 1.0, 0.0
    ).astype(BF16)

    def gates(j, carry):
        z = zn[:, tile(j)]
        sig = sigmoid(dot(w_in_t[512:640], z))
        c_t = cells_in(cot, j)
        c_sig = c_t * sig
        d_p = c_sig.astype(BF16)
        dproj[:, tile(j)] = d_p
        upper[j] = c_sig * (1.0 - sig)
        grad = dot(w_out[...], d_p) * go[...]
        h[j] = grad
        h_mean[j] = mean0(grad)
        return carry

    lax.fori_loop(0, 8, gates, 0, unroll=2)

    def flat(x):
        return x.astype(F32).reshape(64, 128).astype(BF16)

    settle(r1, sems.at[1])

    for side, matrix in ((0, m_left), (1, m_right)):
        for quad in range(4):
            x = jnp.concatenate([flat(r1[:, 4 * quad + k, side]) for k in range(4)], axis=1)
            y = dot(x, lane_swap[...]).astype(BF16)
            for k in range(4):
                matrix[64 * k : 64 * k + 64, 128 * quad : 128 * quad + 128] = y[
                    :, 128 * k : 128 * k + 128
                ]

    def columns(which):
        return m_left[:, pl.ds(pl.multiple_of(which * 256, 256), 256)]

    part_out[...] = dot_tn(columns(1 - core), m_right[...]).astype(BF16)
    swap = pltpu.make_async_remote_copy(
        part_out, part_in, sems.at[2], sems.at[3], device_id=device(partner), device_id_type=MESH
    )
    swap.start()
    part[...] = dot_tn(columns(core), m_right[...])
    swap.wait_recv()
    part[...] = part[...] + part_in[...].astype(F32)
    product = part.reshape(8, 4, 8, 512)

    for quad in range(4):
        lanes = slice(128 * quad, 128 * quad + 128)
        x = jnp.concatenate(
            [product[:, k, :, lanes].reshape(64, 128).astype(BF16) for k in range(4)], axis=1
        )
        y = dot(x, lane_swap[...])
        for k in range(4):
            s2[:, 4 * quad + k] = y[:, 128 * k : 128 * k + 128].reshape(8, 8, 128).astype(BF16)

    to_cells(s2, r2, 4)
    settle(r2, sems.at[5])

    def to_tile_rows(src, dst):
        for g in range(8):
            x = src(g).astype(F32).reshape(128, 128).astype(BF16)
            y = dot(to_tiles, x)
            for j in range(8):
                dst[j, 16 * g : 16 * g + 16, :] = y[16 * j : 16 * j + 16]

    to_tile_rows(lambda g: r2[16 * g : 16 * g + 16], tri)

    def middle(j, carry):
        that, inverse = normalize(tri[j])
        o = (that * go[...]).astype(BF16)
        onorm[:, tile(j)] = o
        dlin[512:640, tile(j)] = (upper[j] * dot(w_out_t[...], o)).astype(BF16)
        grad = h[j]
        d_t = inverse * (grad - h_mean[j] - that * mean0(grad * that))
        dtri[j] = d_t.astype(BF16)
        return carry

    lax.fori_loop(0, 8, middle, 0, unroll=2)

    for g in range(8):
        s3[16 * g : 16 * g + 16] = to_blocks(dtri, g)
    to_chips(s3, r3, 6)

    def fill(dst, base, value):
        for i in range(16):
            dst[base + 2 * i] = value[8 * i : 8 * i + 4]
            dst[base + 2 * i + 1] = value[8 * i + 4 : 8 * i + 8]

    def scatter(src, dst, count, owner, start, k):
        def step(s, carry):
            m = wrap(start + s, count)
            send(src.at[m], dst.at[me], sems.at[k], sems.at[k + 1], owner(m), me)
            return carry

        lax.fori_loop(0, count, step, 0)

    def gather(held, total, dst, m, k):
        total[...] = jnp.sum(held[...], axis=0)

        def step(s, carry):
            send(total, dst.at[m], sems.at[k], sems.at[k + 1], wrap(me + s, 256), me)
            return carry

        lax.fori_loop(0, 256, step, 0)

    fill(g_early, 0, dot_nt(onorm[...], dproj[...]))
    fill(g_early, 32, dot_nt(zn[...], dlin[512:640]))
    early_mine = lax.rem(me, 4) == 3
    scatter(g_early, h_early, 64, lambda m: 4 * m + 3, me // 4, 8)

    settle(r3, sems.at[7])
    for quad in range(4):
        x = jnp.concatenate([flat(r3[:, 4 * quad + k]) for k in range(4)], axis=1)
        y = dot(x, lane_swap[...])
        for k in range(4):
            dtri_f[:, k, :, 128 * quad : 128 * quad + 128] = y[:, 128 * k : 128 * k + 128].reshape(
                8, 8, 128
            )
    dtri_all[core] = dtri_f[...].reshape(256, 512).astype(BF16)
    swap2 = pltpu.make_async_remote_copy(
        dtri_all.at[core], dtri_all.at[core], sems.at[10], sems.at[11],
        device_id=device(partner), device_id_type=MESH,
    )
    swap2.start()
    swap2.wait_recv()
    d_all = dtri_all[...].reshape(512, 512)

    def leave(grad, side):
        for quad in range(4):
            x = jnp.concatenate(
                [
                    grad[64 * k : 64 * k + 64, 128 * quad : 128 * quad + 128]
                    for k in range(4)
                ],
                axis=1,
            )
            y = dot(x, lane_swap[...])
            for k in range(4):
                s4[:, 4 * quad + k, side] = (
                    y[:, 128 * k : 128 * k + 128].reshape(8, 8, 128).astype(BF16)
                )

    leave(dot_nt(m_right[...], d_all).astype(BF16), 0)
    leave(dot(m_left[...], d_all).astype(BF16), 1)
    to_cells(s4, r4, 12)

    @pl.when(early_mine)
    def _():
        settle(h_early, sems.at[9])
        gather(h_early, o_early, a_early, me // 4, 14)

    settle(r4, sems.at[13])
    to_tile_rows(lambda g: r4[16 * g : 16 * g + 16, 0], grad_l)
    to_tile_rows(lambda g: r4[16 * g : 16 * g + 16, 1], grad_r)

    def back(j, carry):
        d_l = grad_l[j]
        d_r = grad_r[j]
        dlin[0:128, tile(j)] = (d_l * a_left[j]).astype(BF16)
        dlin[128:256, tile(j)] = (d_l * b_left[j]).astype(BF16)
        dlin[256:384, tile(j)] = (d_r * a_right[j]).astype(BF16)
        dlin[384:512, tile(j)] = (d_r * b_right[j]).astype(BF16)
        return carry

    lax.fori_loop(0, 8, back, 0, unroll=2)
    sums = dot_nt(zn[...], dlin[0:512])
    for b in range(4):
        fill(g_late, 32 * b, sums[:, 128 * b : 128 * b + 128])
    late_mine = lax.rem(me, 2) == lax.rem(me // 2, 2)
    scatter(g_late, h_late, 128, lambda m: 2 * m + lax.rem(m, 2), chip, 16)

    def finish(j, carry):
        g = dot(w_in[...], dlin[:, tile(j)]) * gi[...]
        normed = zhat[j]
        d = s_z[j] * (g - mean0(g) - normed * mean0(g * normed))
        d = d.T
        for k in range(4):
            d_pair[8 * k + j] = d[32 * k : 32 * k + 32]
        return carry

    lax.fori_loop(0, 8, finish, 0, unroll=2)

    @pl.when(late_mine)
    def _():
        settle(h_late, sems.at[17])
        gather(h_late, o_late, a_late, chip, 18)

    def collect(dst, lanes, src, base):
        for i in range(16):
            dst[8 * i : 8 * i + 4, lanes] = src[base + 2 * i] * scale
            dst[8 * i + 4 : 8 * i + 8, lanes] = src[base + 2 * i + 1] * scale

    settle(a_early, sems.at[15])
    collect(d_w_out, slice(0, 128), a_early, 0)
    collect(d_w_in, slice(512, 640), a_early, 32)
    settle(a_late, sems.at[19])
    for b in range(4):
        collect(d_w_in, slice(128 * b, 128 * b + 128), a_late, 32 * b)
    weighted = d_w_in[...] * w_in[...].astype(F32)
    folded = weighted[:, 0:128]
    for b in range(1, 5):
        folded = folded + weighted[:, 128 * b : 128 * b + 128]
    d_gain_in[...] = jnp.sum(folded.T, axis=0, keepdims=True) / gain_in[...]
    weighted = d_w_out[...] * w_out[...].astype(F32)
    d_gain_out[...] = jnp.sum(weighted.T, axis=0, keepdims=True) / gain_out[...]

    sent(s1, 0)
    swap.wait_send()
    flat_sent = ((r2, 4), (s3, 6), (r4, 12))
    for ref, k in flat_sent:
        sent(ref, k)
    swap2.wait_send()
    settle(g_early.at[pl.ds(0, 63)], sems.at[8])

    @pl.when(jnp.logical_not(early_mine))
    def _():
        settle(g_early.at[0], sems.at[8])

    @pl.when(early_mine)
    def _():
        settle(h_early.at[pl.ds(0, 255)], sems.at[14])

    settle(g_late.at[pl.ds(0, 127)], sems.at[16])

    @pl.when(jnp.logical_not(late_mine))
    def _():
        settle(g_late.at[0], sems.at[16])

    @pl.when(late_mine)
    def _():
        settle(h_late.at[pl.ds(0, 255)], sems.at[18])


def body(pair, pair_mask, proj_weight, out_weight, in_gain, out_gain, cotangent):
    vmem = pl.BlockSpec(memory_space=pltpu.VMEM)
    V = pltpu.VMEM
    tiles = V((8, 128, 128), F32)
    tiles16 = V((8, 128, 128), BF16)
    by_tile = V((8, 1, 128), F32)
    lanes16 = V((128, 1024), BF16)
    scratch = [
        V((128, 2, 8, 128), BF16), V((8, 16, 2, 8, 128), BF16),
        V((8, 16, 8, 128), BF16), V((128, 8, 128), BF16),
        V((128, 8, 128), BF16), V((8, 16, 8, 128), BF16),
        V((8, 16, 2, 8, 128), BF16), V((128, 2, 8, 128), BF16),
        V((512, 512), BF16), by_tile, V((640, 128), BF16), V((128, 128), BF16),
        V((128, 128), F32), V((128, 128), F32),
        tiles, by_tile, lanes16, tiles16, tiles16, tiles, tiles, tiles, tiles, V((8, 128), F32),
        lanes16, tiles, tiles, by_tile, V((256, 512), BF16), V((256, 512), BF16),
        V((256, 512), F32), V((256, 512), BF16), V((256, 512), BF16),
        tiles, lanes16, tiles16, V((8, 4, 8, 512), F32), V((2, 256, 512), BF16),
        tiles, tiles, V((640, 1024), BF16),
        V((64, 4, 128), F32), V((256, 4, 128), F32), V((4, 128), F32), V((64, 4, 128), F32),
        V((128, 4, 128), F32), V((256, 4, 128), F32), V((4, 128), F32), V((128, 4, 128), F32),
        pltpu.SemaphoreType.DMA((20,)),
    ]
    outs = pl.pallas_call(
        kernel,
        out_shape=(
            jax.ShapeDtypeStruct(pair.shape, F32),
            jax.ShapeDtypeStruct((128, 640), F32),
            jax.ShapeDtypeStruct((128, 128), F32),
            jax.ShapeDtypeStruct((1, 128), F32),
            jax.ShapeDtypeStruct((1, 128), F32),
        ),
        in_specs=[vmem] * 7,
        out_specs=[vmem] * 5,
        scratch_shapes=scratch,
        name="triangle_back",
        compiler_params=pltpu.CompilerParams(collective_id=0, has_side_effects=True),
    )(
        pair, pair_mask, proj_weight, out_weight,
        in_gain.reshape(1, 128), out_gain.reshape(1, 128), cotangent,
    )
    return (*outs[:3], outs[3].reshape(128), outs[4].reshape(128))


def solution(mesh):
    in_specs = (P("row", "col", None), P("row", "col"), P(), P(), P(), P(), P("row", "col", None))
    out_specs = (P("row", "col", None), P(), P(), P(), P())
    return jax.shard_map(body, mesh=mesh, in_specs=in_specs, out_specs=out_specs, check_vma=False)
```

time: 760 us -> 117 us (0.15)
  waiting for transfers between devices: 582 us -> 0 us
  Pallas kernels: 0 us -> 112 us
  blocking collectives: 77 us -> 0 us
  local copies, waits for them, and re-layouts: 40.6 us -> 4.53 us
  matrix products: 26 us -> 0 us
  other arithmetic: 18.9 us -> 0 us
  between operations: 14 us -> 0.66 us
    psum x1 -> x0, waiting for transfers between devices: 246 us -> none  [body(): lax.psum((proj_local, out_weight_local, in_gain_local, out_gain_local), (...]
    reduce_scatter x2 -> x0, waiting for transfers between devices: 174 us -> none  [the longest x1 95.7 us: body(): lax.psum_scatter(jnp.einsum('kic,kjc->ijc', piece, right, preferred_eleme...]
    all_gather x2 -> x0, waiting for transfers between devices: 162 us -> none  [the longest x1 98.2 us: body(): do_panels = lax.all_gather(dtri, 'row', axis=0, tiled=True)]
    pallas_call x0 -> x1, Pallas kernels: none -> 112 us  [body(): pl.pallas_call(kernel, out_shape=(jax.ShapeDtypeStruct(pair.shape, F32),...]
    psum x1 -> x0, blocking collectives: 77 us -> none  [body(): lax.psum((proj_local, out_weight_local, in_gain_local, out_gain_local), (...]
    dot_general x9 -> x0, matrix products: 26 us -> none  [the longest x1 6.06 us: body(): jnp.einsum('kic,ijc->kjc', panels, do_panels, preferred_element_type=jnp....]
    dot_general x3 -> x0, local copies, waits for them, and re-layouts: 19.9 us -> none  [the longest x1 9.17 us: body(): jnp.einsum('kic,kjc->ijc', piece, right, preferred_element_type=jnp.float32)]
    all_gather x2 -> x0, local copies, waits for them, and re-layouts: 16.6 us -> none  [the longest x1 8.6 us: body(): do_panels = lax.all_gather(dtri, 'row', axis=0, tiled=True)]
  transfers between devices with their start and end apart: 5 -> 0, of which waited for: 5 -> 0; matrix products, arithmetic and copies ran while one was open for 2% -> 0% of each run, Pallas kernels for 0% -> 0%
where the time goes in v3:
time: 117 us
  Pallas kernels  112 us (96%)
  local copies, waits for them, and re-layouts  4.53 us (4%)
    pallas_call x1, Pallas kernels, body(): pl.pallas_call(kernel, out_shape=(jax.ShapeDtypeStruct(pair.shape, F32),...  112 us
    unnamed x13, local copies, waits for them, and re-layouts  4.53 us

profile of v3, /device:TPU:1, one launch (start us, length us, event | category | flops | bytes accessed | tf_op | source)
XLA Modules:
  0.0 117.2 jit_solution(1666907978809899873)
XLA Ops:
  0.6 112.0 %triangle_back.1 = (f32[32,32,128]{2,1,0:T(8,128)}, f32[128,640]{1,0:T(8,128)}, f32[128,128]{1,0:T(8,128)}, f32[1,128]{1,0:T(1,128)}, f32[1,128]{1,0:T(1,128)}) custom-call(bf16[32,32,128]{2,1,0:T(8,128)(2,1)} %pair.1, s32[32,32]{1,0:T(8,128)} %mask.1, bf16[128,640]{1,0:T(8,128)(2,1)} %w_in.1, bf16[128,128]{1,0:T(8,128)(2,1)} %w_out.1, f32[1,128]{1,0:T(1,128)} %bitcast.4, ...), custom_call_target="tpu_custom_call" | custom-call | tf_op jit(solution)/shard_map/triangle_back/pallas_call | solution.py:443
  112.7 0.0 copy-start
  112.7 1.9 %copy.17 = f32[32,32,128]{2,1,0:T(8,128)} copy(f32[32,32,128]{2,1,0:T(8,128)} %get-tuple-element.20) | data formatting | bytes 1048576
  114.6 0.0 copy-done
  114.6 0.0 copy-start.1
  114.6 0.7 copy.18
  115.3 0.1 copy-done.1
  115.5 0.0 copy-start.3
  115.5 0.6 copy.19
  116.1 0.0 copy-done.3
  116.1 0.0 copy-start.2
  116.1 0.5 copy.20
  116.6 0.1 copy-done.2
  116.7 0.5 copy.21
Async XLA Ops:
  112.7 1.9 %copy-start = (f32[128,640]{1,0:T(8,128)S(1)}, f32[128,640]{1,0:T(8,128)}, u32[]{:S(2)}) copy-start(f32[128,640]{1,0:T(8,128)} %get-tuple-element.21) | copy-start | bytes 983044
  114.6 0.9 copy-start.1
  115.5 0.6 copy-start.3
  116.1 0.6 copy-start.2

commit v4 on v3

--- a/solution.py
+++ b/solution.py
@@ -15,10 +15,6 @@
     pltpu.make_async_copy(ref, ref, sem).wait()
 
 
-def device(number):
-    return (number // 16, lax.rem(number, 16))
-
-
 def wrap(value, size):
     return jnp.where(value >= size, value - size, value)
 
@@ -49,27 +45,31 @@
     return 1.0 / (1.0 + jnp.exp(-x))
 
 
-def send(src, dst, send_sem, recv_sem, number, me):
-    @pl.when(number != me)
-    def _():
-        pltpu.make_async_remote_copy(
-            src, dst, send_sem, recv_sem, device_id=device(number), device_id_type=MESH
-        ).start()
-
-    @pl.when(number == me)
+def start(src, dst, send_sem, recv_sem, row, col):
+    pltpu.make_async_remote_copy(
+        src, dst, send_sem, recv_sem, device_id=(row, col), device_id_type=MESH
+    ).start()
+
+
+def keep_or_start(mine, src, dst, send_sem, recv_sem, row, col):
+    @pl.when(mine)
     def _():
         pltpu.make_async_copy(src, dst, recv_sem).start()
+
+    @pl.when(jnp.logical_not(mine))
+    def _():
+        start(src, dst, send_sem, recv_sem, row, col)
 
 
 def kernel(
     pair, mask, w_in, w_out, gain_in, gain_out, cot,
     d_pair, d_w_in, d_w_out, d_gain_in, d_gain_out,
-    s1, r1, s2, r2, s3, r3, s4, r4,
+    s1, r1, s2, r2, s3, r3, s4l, s4r, r4l, r4r,
     lane_swap, cell_mask, w_in_t, w_out_t, gi, go,
     zhat, s_z, zn, left, right, a_left, b_left, a_right, b_right, gate,
     dproj, upper, h, h_mean, m_left, m_right, part, part_out, part_in,
     tri, onorm, dtri, dtri_f, dtri_all, grad_l, grad_r, dlin,
-    g_early, h_early, o_early, a_early, g_late, h_late, o_late, a_late,
+    g_early, h_early, o_early, a_early, g_l, h_l, o_l, a_l, g_r, h_r, o_r, a_r,
     sems,
 ):
     row = lax.axis_index("row")
@@ -80,19 +80,26 @@
     half = row // 8
     row8 = lax.rem(row, 8)
     cell = row8 * 16 + col
-    partner = me + 1 - 2 * core
-    own = 1 - lax.rem(half + core, 2)
+    seat = col // 2
+    beside = (row, col + 1 - 2 * core)
+    mine = half == core
     scale = 1.0 / 512.0
-
     barrier = pltpu.get_barrier_semaphore()
 
-    def hello(s, carry):
-        pl.semaphore_signal(
-            barrier, inc=1, device_id=device(wrap(me + s, 256)), device_id_type=MESH
-        )
+    def hello(a, first=0):
+        to_row = wrap(row + a, 16)
+        for b in range(first, 16):
+            pl.semaphore_signal(
+                barrier, inc=1, device_id=(to_row, wrap(col + b, 16)), device_id_type=MESH
+            )
+
+    def hello_row(a, carry):
+        hello(a)
         return carry
 
-    lax.fori_loop(1, 256, hello, 0)
+    lax.fori_loop(7, 16, hello_row, 0)
+    lax.fori_loop(1, 7, hello_row, 0)
+    hello(0, 1)
 
     def iota(shape, axis):
         return lax.broadcasted_iota(jnp.int32, shape, axis)
@@ -156,28 +163,52 @@
     pl.semaphore_wait(barrier, 255)
 
     def to_chips(src, dst, k):
-        def step(s, carry):
-            c = wrap(chip + s, 128)
-            send(src.at[c], dst.at[row8, col], sems.at[k], sems.at[k + 1], 2 * c + half, me)
+        there = dst.at[row8, col]
+
+        def ring(a, first=0):
+            to_row = wrap(row + a, 16)
+            for b in range(first, 8):
+                to_seat = wrap(seat + b, 8)
+                start(
+                    src.at[to_row * 8 + to_seat], there, sems.at[k], sems.at[k + 1],
+                    to_row, 2 * to_seat + half,
+                )
+
+        def step(a, carry):
+            ring(a)
             return carry
 
-        lax.fori_loop(0, 128, step, 0)
+        keep_or_start(mine, src.at[chip], there, sems.at[k], sems.at[k + 1], *beside)
+        ring(0, 1)
+        lax.fori_loop(1, 16, step, 0)
 
     def to_cells(src, dst, k):
-        def step(s, carry):
-            t = wrap(cell + s, 128)
-            send(
-                src.at[t // 16, lax.rem(t, 16)], dst.at[chip], sems.at[k], sems.at[k + 1],
-                core * 128 + t, me,
-            )
+        there = dst.at[chip]
+        base = core * 8
+
+        def ring(a, first=0):
+            block = wrap(row8 + a, 8)
+            for b in range(first, 16):
+                to_col = wrap(col + b, 16)
+                start(
+                    src.at[block, to_col], there, sems.at[k], sems.at[k + 1],
+                    base + block, to_col,
+                )
+
+        def step(a, carry):
+            ring(a)
             return carry
 
-        lax.fori_loop(0, 128, step, 0)
+        keep_or_start(
+            mine, src.at[row8, col], there, sems.at[k], sems.at[k + 1], base + row8, col
+        )
+        ring(0, 1)
+        lax.fori_loop(1, 8, step, 0)
 
     def sent(ref, k):
         settle(ref.at[pl.ds(0, 127)], sems.at[k])
 
-        @pl.when(own == 0)
+        @pl.when(jnp.logical_not(mine))
         def _():
             settle(ref.at[0], sems.at[k])
 
@@ -222,7 +253,7 @@
 
     part_out[...] = dot_tn(columns(1 - core), m_right[...]).astype(BF16)
     swap = pltpu.make_async_remote_copy(
-        part_out, part_in, sems.at[2], sems.at[3], device_id=device(partner), device_id_type=MESH
+        part_out, part_in, sems.at[2], sems.at[3], device_id=beside, device_id_type=MESH
     )
     swap.start()
     part[...] = dot_tn(columns(core), m_right[...])
@@ -267,32 +298,77 @@
         s3[16 * g : 16 * g + 16] = to_blocks(dtri, g)
     to_chips(s3, r3, 6)
 
-    def fill(dst, base, value):
-        for i in range(16):
-            dst[base + 2 * i] = value[8 * i : 8 * i + 4]
-            dst[base + 2 * i + 1] = value[8 * i + 4 : 8 * i + 8]
-
-    def scatter(src, dst, count, owner, start, k):
-        def step(s, carry):
-            m = wrap(start + s, count)
-            send(src.at[m], dst.at[me], sems.at[k], sems.at[k + 1], owner(m), me)
+    def fill(dst, value):
+        rows = value.astype(BF16)
+        for b in range(2):
+            for i in range(64):
+                dst[64 * b + i] = rows[2 * i : 2 * i + 2, 128 * b : 128 * b + 128]
+
+    def owner(to_seat, flip):
+        return lax.rem(to_seat + flip, 2)
+
+    def scatter(src, dst, flip, k):
+        there = dst.at[me]
+
+        def ring(a, first=0):
+            to_row = wrap(row + a, 16)
+            for b in range(first, 8):
+                to_seat = wrap(seat + b, 8)
+                start(
+                    src.at[to_row * 8 + to_seat], there, sems.at[k], sems.at[k + 1],
+                    to_row, 2 * to_seat + owner(to_seat, flip),
+                )
+
+        def step(a, carry):
+            ring(a)
             return carry
 
-        lax.fori_loop(0, count, step, 0)
-
-    def gather(held, total, dst, m, k):
-        total[...] = jnp.sum(held[...], axis=0)
-
-        def step(s, carry):
-            send(total, dst.at[m], sems.at[k], sems.at[k + 1], wrap(me + s, 256), me)
-            return carry
-
-        lax.fori_loop(0, 256, step, 0)
-
-    fill(g_early, 0, dot_nt(onorm[...], dproj[...]))
-    fill(g_early, 32, dot_nt(zn[...], dlin[512:640]))
-    early_mine = lax.rem(me, 4) == 3
-    scatter(g_early, h_early, 64, lambda m: 4 * m + 3, me // 4, 8)
+        keep_or_start(
+            owner(seat, flip) == core, src.at[chip], there, sems.at[k], sems.at[k + 1], *beside
+        )
+        ring(0, 1)
+        lax.fori_loop(1, 16, step, 0)
+
+    def gather(held, total, dst, flip, k):
+        @pl.when(owner(seat, flip) == core)
+        def _():
+            settle(held, sems.at[k + 1])
+            total[...] = jnp.sum(held[...].astype(F32), axis=0).astype(BF16)
+            there = dst.at[chip]
+
+            def ring(a, first=0):
+                to_row = wrap(row + a, 16)
+                for b in range(first, 16):
+                    start(
+                        total, there, sems.at[k + 2], sems.at[k + 3],
+                        to_row, wrap(col + b, 16),
+                    )
+
+            def step(a, carry):
+                ring(a)
+                return carry
+
+            pltpu.make_async_copy(total, there, sems.at[k + 3]).start()
+            ring(0, 1)
+            lax.fori_loop(1, 16, step, 0)
+
+    def finished(src, held, flip, k):
+        settle(src.at[pl.ds(0, 127)], sems.at[k])
+
+        @pl.when(owner(seat, flip) != core)
+        def _():
+            settle(src.at[0], sems.at[k])
+
+        @pl.when(owner(seat, flip) == core)
+        def _():
+            settle(held.at[pl.ds(0, 255)], sems.at[k + 2])
+
+    fill(
+        g_early,
+        jnp.concatenate(
+            [dot_nt(onorm[...], dproj[...]), dot_nt(zn[...], dlin[512:640])], axis=1
+        ),
+    )
 
     settle(r3, sems.at[7])
     for quad in range(4):
@@ -305,13 +381,13 @@
     dtri_all[core] = dtri_f[...].reshape(256, 512).astype(BF16)
     swap2 = pltpu.make_async_remote_copy(
         dtri_all.at[core], dtri_all.at[core], sems.at[10], sems.at[11],
-        device_id=device(partner), device_id_type=MESH,
+        device_id=beside, device_id_type=MESH,
     )
     swap2.start()
     swap2.wait_recv()
     d_all = dtri_all[...].reshape(512, 512)
 
-    def leave(grad, side):
+    def leave(grad, dst):
         for quad in range(4):
             x = jnp.concatenate(
                 [
@@ -322,38 +398,39 @@
             )
             y = dot(x, lane_swap[...])
             for k in range(4):
-                s4[:, 4 * quad + k, side] = (
+                dst[:, 4 * quad + k] = (
                     y[:, 128 * k : 128 * k + 128].reshape(8, 8, 128).astype(BF16)
                 )
 
-    leave(dot_nt(m_right[...], d_all).astype(BF16), 0)
-    leave(dot(m_left[...], d_all).astype(BF16), 1)
-    to_cells(s4, r4, 12)
-
-    @pl.when(early_mine)
-    def _():
-        settle(h_early, sems.at[9])
-        gather(h_early, o_early, a_early, me // 4, 14)
-
-    settle(r4, sems.at[13])
-    to_tile_rows(lambda g: r4[16 * g : 16 * g + 16, 0], grad_l)
-    to_tile_rows(lambda g: r4[16 * g : 16 * g + 16, 1], grad_r)
-
-    def back(j, carry):
-        d_l = grad_l[j]
-        d_r = grad_r[j]
-        dlin[0:128, tile(j)] = (d_l * a_left[j]).astype(BF16)
-        dlin[128:256, tile(j)] = (d_l * b_left[j]).astype(BF16)
-        dlin[256:384, tile(j)] = (d_r * a_right[j]).astype(BF16)
-        dlin[384:512, tile(j)] = (d_r * b_right[j]).astype(BF16)
-        return carry
-
-    lax.fori_loop(0, 8, back, 0, unroll=2)
-    sums = dot_nt(zn[...], dlin[0:512])
-    for b in range(4):
-        fill(g_late, 32 * b, sums[:, 128 * b : 128 * b + 128])
-    late_mine = lax.rem(me, 2) == lax.rem(me // 2, 2)
-    scatter(g_late, h_late, 128, lambda m: 2 * m + lax.rem(m, 2), chip, 16)
+    leave(dot_nt(m_right[...], d_all).astype(BF16), s4l)
+    to_cells(s4l, r4l, 12)
+    leave(dot(m_left[...], d_all).astype(BF16), s4r)
+    to_cells(s4r, r4r, 14)
+    scatter(g_early, h_early, 1, 16)
+
+    def back(grad, value, slope, base):
+        def step(j, carry):
+            d = grad[j]
+            dlin[base : base + 128, tile(j)] = (d * value[j]).astype(BF16)
+            dlin[base + 128 : base + 256, tile(j)] = (d * slope[j]).astype(BF16)
+            return carry
+
+        lax.fori_loop(0, 8, step, 0, unroll=2)
+
+    settle(r4l, sems.at[13])
+    to_tile_rows(lambda g: r4l[16 * g : 16 * g + 16], grad_l)
+    back(grad_l, a_left, b_left, 0)
+    fill(g_l, dot_nt(zn[...], dlin[0:256]))
+    scatter(g_l, h_l, 0, 20)
+
+    settle(r4r, sems.at[15])
+    to_tile_rows(lambda g: r4r[16 * g : 16 * g + 16], grad_r)
+    back(grad_r, a_right, b_right, 256)
+    fill(g_r, dot_nt(zn[...], dlin[256:512]))
+    scatter(g_r, h_r, 1, 24)
+
+    gather(h_early, o_early, a_early, 1, 16)
+    gather(h_l, o_l, a_l, 0, 20)
 
     def finish(j, carry):
         g = dot(w_in[...], dlin[:, tile(j)]) * gi[...]
@@ -364,57 +441,41 @@
             d_pair[8 * k + j] = d[32 * k : 32 * k + 32]
         return carry
 
-    lax.fori_loop(0, 8, finish, 0, unroll=2)
-
-    @pl.when(late_mine)
-    def _():
-        settle(h_late, sems.at[17])
-        gather(h_late, o_late, a_late, chip, 18)
+    lax.fori_loop(0, 4, finish, 0, unroll=2)
+    gather(h_r, o_r, a_r, 1, 24)
+    lax.fori_loop(4, 8, finish, 0, unroll=2)
 
     def collect(dst, lanes, src, base):
-        for i in range(16):
-            dst[8 * i : 8 * i + 4, lanes] = src[base + 2 * i] * scale
-            dst[8 * i + 4 : 8 * i + 8, lanes] = src[base + 2 * i + 1] * scale
-
-    settle(a_early, sems.at[15])
+        for i in range(64):
+            dst[2 * i : 2 * i + 2, lanes] = src[base + i].astype(F32) * scale
+
+    settle(a_early, sems.at[19])
     collect(d_w_out, slice(0, 128), a_early, 0)
-    collect(d_w_in, slice(512, 640), a_early, 32)
-    settle(a_late, sems.at[19])
-    for b in range(4):
-        collect(d_w_in, slice(128 * b, 128 * b + 128), a_late, 32 * b)
+    collect(d_w_in, slice(512, 640), a_early, 64)
+    weighted = d_w_out[...] * w_out[...].astype(F32)
+    d_gain_out[...] = jnp.sum(weighted.T, axis=0, keepdims=True) / gain_out[...]
+    settle(a_l, sems.at[23])
+    collect(d_w_in, slice(0, 128), a_l, 0)
+    collect(d_w_in, slice(128, 256), a_l, 64)
+    settle(a_r, sems.at[27])
+    collect(d_w_in, slice(256, 384), a_r, 0)
+    collect(d_w_in, slice(384, 512), a_r, 64)
     weighted = d_w_in[...] * w_in[...].astype(F32)
     folded = weighted[:, 0:128]
     for b in range(1, 5):
         folded = folded + weighted[:, 128 * b : 128 * b + 128]
     d_gain_in[...] = jnp.sum(folded.T, axis=0, keepdims=True) / gain_in[...]
-    weighted = d_w_out[...] * w_out[...].astype(F32)
-    d_gain_out[...] = jnp.sum(weighted.T, axis=0, keepdims=True) / gain_out[...]
 
     sent(s1, 0)
     swap.wait_send()
-    flat_sent = ((r2, 4), (s3, 6), (r4, 12))
-    for ref, k in flat_sent:
-        sent(ref, k)
+    sent(r2, 4)
+    sent(s3, 6)
     swap2.wait_send()
-    settle(g_early.at[pl.ds(0, 63)], sems.at[8])
-
-    @pl.when(jnp.logical_not(early_mine))
-    def _():
-        settle(g_early.at[0], sems.at[8])
-
-    @pl.when(early_mine)
-    def _():
-        settle(h_early.at[pl.ds(0, 255)], sems.at[14])
-
-    settle(g_late.at[pl.ds(0, 127)], sems.at[16])
-
-    @pl.when(jnp.logical_not(late_mine))
-    def _():
-        settle(g_late.at[0], sems.at[16])
-
-    @pl.when(late_mine)
-    def _():
-        settle(h_late.at[pl.ds(0, 255)], sems.at[18])
+    sent(r4l, 12)
+    sent(r4r, 14)
+    finished(g_early, h_early, 1, 16)
+    finished(g_l, h_l, 0, 20)
+    finished(g_r, h_r, 1, 24)
 
 
 def body(pair, pair_mask, proj_weight, out_weight, in_gain, out_gain, cotangent):
@@ -424,11 +485,13 @@
     tiles16 = V((8, 128, 128), BF16)
     by_tile = V((8, 1, 128), F32)
     lanes16 = V((128, 1024), BF16)
+    sums = (V((128, 2, 128), BF16), V((256, 2, 128), BF16), V((2, 128), BF16), V((128, 2, 128), BF16))
     scratch = [
         V((128, 2, 8, 128), BF16), V((8, 16, 2, 8, 128), BF16),
         V((8, 16, 8, 128), BF16), V((128, 8, 128), BF16),
         V((128, 8, 128), BF16), V((8, 16, 8, 128), BF16),
-        V((8, 16, 2, 8, 128), BF16), V((128, 2, 8, 128), BF16),
+        V((8, 16, 8, 128), BF16), V((8, 16, 8, 128), BF16),
+        V((128, 8, 128), BF16), V((128, 8, 128), BF16),
         V((512, 512), BF16), by_tile, V((640, 128), BF16), V((128, 128), BF16),
         V((128, 128), F32), V((128, 128), F32),
         tiles, by_tile, lanes16, tiles16, tiles16, tiles, tiles, tiles, tiles, V((8, 128), F32),
@@ -436,9 +499,8 @@
         V((256, 512), F32), V((256, 512), BF16), V((256, 512), BF16),
         tiles, lanes16, tiles16, V((8, 4, 8, 512), F32), V((2, 256, 512), BF16),
         tiles, tiles, V((640, 1024), BF16),
-        V((64, 4, 128), F32), V((256, 4, 128), F32), V((4, 128), F32), V((64, 4, 128), F32),
-        V((128, 4, 128), F32), V((256, 4, 128), F32), V((4, 128), F32), V((128, 4, 128), F32),
-        pltpu.SemaphoreType.DMA((20,)),
+        *sums, *sums, *sums,
+        pltpu.SemaphoreType.DMA((28,)),
     ]
     outs = pl.pallas_call(
         kernel,

time: 117 us -> 101 us (0.86)
  Pallas kernels: 112 us -> 95.7 us
    pallas_call x1, Pallas kernels: 112 us -> 95.7 us  [body(): pl.pallas_call(kernel, out_shape=(jax.ShapeDtypeStruct(pair.shape, F32),...]
where the time goes in v4:
time: 101 us
  Pallas kernels  95.7 us (95%)
  local copies, waits for them, and re-layouts  4.53 us (4%)
    pallas_call x1, Pallas kernels, body(): pl.pallas_call(kernel, out_shape=(jax.ShapeDtypeStruct(pair.shape, F32),...  95.7 us
    unnamed x13, local copies, waits for them, and re-layouts  4.53 us

profile of v4, /device:TPU:1, one launch (start us, length us, event | category | flops | bytes accessed | tf_op | source)
XLA Modules:
  0.0 100.9 jit_solution(812240756101361194)
XLA Ops:
  0.6 95.7 %triangle_back.1 = (f32[32,32,128]{2,1,0:T(8,128)}, f32[128,640]{1,0:T(8,128)}, f32[128,128]{1,0:T(8,128)}, f32[1,128]{1,0:T(1,128)}, f32[1,128]{1,0:T(1,128)}) custom-call(bf16[32,32,128]{2,1,0:T(8,128)(2,1)} %pair.1, s32[32,32]{1,0:T(8,128)} %mask.1, bf16[128,640]{1,0:T(8,128)(2,1)} %w_in.1, bf16[128,128]{1,0:T(8,128)(2,1)} %w_out.1, f32[1,128]{1,0:T(1,128)} %bitcast.4, ...), custom_call_target="tpu_custom_call" | custom-call | tf_op jit(solution)/shard_map/triangle_back/pallas_call | solution.py:505
  96.3 0.0 copy-start
  96.3 1.9 %copy.17 = f32[32,32,128]{2,1,0:T(8,128)} copy(f32[32,32,128]{2,1,0:T(8,128)} %get-tuple-element.20) | data formatting | bytes 1048576
  98.3 0.0 copy-done
  98.3 0.0 copy-start.1
  98.3 0.7 copy.18
  99.0 0.1 copy-done.1
  99.1 0.0 copy-start.3
  99.1 0.6 copy.19
  99.8 0.0 copy-done.3
  99.8 0.0 copy-start.2
  99.8 0.5 copy.20
  100.3 0.1 copy-done.2
  100.4 0.5 copy.21
Async XLA Ops:
  96.3 1.9 %copy-start = (f32[128,640]{1,0:T(8,128)S(1)}, f32[128,640]{1,0:T(8,128)}, u32[]{:S(2)}) copy-start(f32[128,640]{1,0:T(8,128)} %get-tuple-element.21) | copy-start | bytes 983044
  98.3 0.9 copy-start.1
  99.1 0.6 copy-start.3
  99.8 0.6 copy-start.2

commit v5 on v4

--- a/solution.py
+++ b/solution.py
@@ -62,15 +62,16 @@
 
 
 def kernel(
-    pair, mask, w_in, w_out, gain_in, gain_out, cot,
-    d_pair, d_w_in, d_w_out, d_gain_in, d_gain_out,
-    s1, r1, s2, r2, s3, r3, s4l, s4r, r4l, r4r,
+    pair_h, mask_h, w_in_h, w_out_h, gain_in_h, gain_out_h, cot_h,
+    d_pair_h, d_w_in, d_w_out, d_gain_in, d_gain_out,
+    s1l, s1r, r1l, r1r, s2, r2, s3, r3, s4l, s4r, r4l, r4r,
     lane_swap, cell_mask, w_in_t, w_out_t, gi, go,
-    zhat, s_z, zn, left, right, a_left, b_left, a_right, b_right, gate,
+    zhat, s_z, zn, left, right, a_left, b_left, a_right, b_right,
     dproj, upper, h, h_mean, m_left, m_right, part, part_out, part_in,
     tri, onorm, dtri, dtri_f, dtri_all, grad_l, grad_r, dlin,
     g_early, h_early, o_early, a_early, g_l, h_l, o_l, a_l, g_r, h_r, o_r, a_r,
-    sems,
+    pair, mask, w_in, w_out, gain_in, gain_out, cot, d_pair,
+    local_sems, sems,
 ):
     row = lax.axis_index("row")
     col = lax.axis_index("col")
@@ -84,6 +85,17 @@
     beside = (row, col + 1 - 2 * core)
     mine = half == core
     scale = 1.0 / 512.0
+    loads = [
+        pltpu.make_async_copy(src, dst, local_sems.at[n])
+        for n, (src, dst) in enumerate(
+            (
+                (w_in_h, w_in), (w_out_h, w_out), (gain_in_h, gain_in), (gain_out_h, gain_out),
+                (mask_h, mask), (pair_h, pair), (cot_h, cot),
+            )
+        )
+    ]
+    for load in loads:
+        load.start()
     barrier = pltpu.get_barrier_semaphore()
 
     def hello(a, first=0):
@@ -108,6 +120,8 @@
     to_block = jnp.where(c_i == (r_i & 7) * 16 + (r_i >> 3), 1.0, 0.0).astype(BF16)
     to_tiles = jnp.where(c_i == (r_i & 15) * 8 + (r_i >> 4), 1.0, 0.0).astype(BF16)
 
+    for load in loads[:6]:
+        load.wait()
     w_in_t[...] = w_in[...].astype(F32).T.astype(BF16)
     w_out_t[...] = w_out[...].astype(F32).T.astype(BF16)
     gi[...] = jnp.broadcast_to(gain_in[...], (128, 128)).T
@@ -157,8 +171,8 @@
         ).astype(BF16)
 
     for g in range(8):
-        s1[16 * g : 16 * g + 16, 0] = to_blocks(left, g)
-        s1[16 * g : 16 * g + 16, 1] = to_blocks(right, g)
+        s1l[16 * g : 16 * g + 16] = to_blocks(left, g)
+        s1r[16 * g : 16 * g + 16] = to_blocks(right, g)
 
     pl.semaphore_wait(barrier, 255)
 
@@ -212,7 +226,8 @@
         def _():
             settle(ref.at[0], sems.at[k])
 
-    to_chips(s1, r1, 0)
+    to_chips(s1l, r1l, 0)
+    to_chips(s1r, r1r, 28)
 
     l_i, l_o = iota((512, 512), 0), iota((512, 512), 1)
     lane_swap[...] = jnp.where(
@@ -232,21 +247,31 @@
         h_mean[j] = mean0(grad)
         return carry
 
+    loads[6].wait()
     lax.fori_loop(0, 8, gates, 0, unroll=2)
 
     def flat(x):
         return x.astype(F32).reshape(64, 128).astype(BF16)
 
-    settle(r1, sems.at[1])
-
-    for side, matrix in ((0, m_left), (1, m_right)):
+    def swapped(piece):
+        x = jnp.concatenate(
+            [
+                jnp.concatenate([piece(quad, k) for k in range(4)], axis=1)
+                for quad in range(4)
+            ],
+            axis=0,
+        )
+        return dot(x, lane_swap[...])
+
+    def part_of(y, quad, k):
+        return y[64 * quad : 64 * quad + 64, 128 * k : 128 * k + 128]
+
+    for side, (landed, matrix) in enumerate(((r1l, m_left), (r1r, m_right))):
+        settle(landed, sems.at[1 + 28 * side])
+        y = swapped(lambda quad, k: flat(landed[:, 4 * quad + k])).astype(BF16)
         for quad in range(4):
-            x = jnp.concatenate([flat(r1[:, 4 * quad + k, side]) for k in range(4)], axis=1)
-            y = dot(x, lane_swap[...]).astype(BF16)
             for k in range(4):
-                matrix[64 * k : 64 * k + 64, 128 * quad : 128 * quad + 128] = y[
-                    :, 128 * k : 128 * k + 128
-                ]
+                matrix[64 * k : 64 * k + 64, 128 * quad : 128 * quad + 128] = part_of(y, quad, k)
 
     def columns(which):
         return m_left[:, pl.ds(pl.multiple_of(which * 256, 256), 256)]
@@ -261,14 +286,13 @@
     part[...] = part[...] + part_in[...].astype(F32)
     product = part.reshape(8, 4, 8, 512)
 
+    def lanes(quad):
+        return slice(128 * quad, 128 * quad + 128)
+
+    y = swapped(lambda quad, k: product[:, k, :, lanes(quad)].reshape(64, 128).astype(BF16))
     for quad in range(4):
-        lanes = slice(128 * quad, 128 * quad + 128)
-        x = jnp.concatenate(
-            [product[:, k, :, lanes].reshape(64, 128).astype(BF16) for k in range(4)], axis=1
-        )
-        y = dot(x, lane_swap[...])
         for k in range(4):
-            s2[:, 4 * quad + k] = y[:, 128 * k : 128 * k + 128].reshape(8, 8, 128).astype(BF16)
+            s2[:, 4 * quad + k] = part_of(y, quad, k).reshape(8, 8, 128).astype(BF16)
 
     to_cells(s2, r2, 4)
     settle(r2, sems.at[5])
@@ -326,8 +350,9 @@
         keep_or_start(
             owner(seat, flip) == core, src.at[chip], there, sems.at[k], sems.at[k + 1], *beside
         )
+        lax.fori_loop(6, 16, step, 0)
+        lax.fori_loop(1, 6, step, 0)
         ring(0, 1)
-        lax.fori_loop(1, 16, step, 0)
 
     def gather(held, total, dst, flip, k):
         @pl.when(owner(seat, flip) == core)
@@ -349,8 +374,9 @@
                 return carry
 
             pltpu.make_async_copy(total, there, sems.at[k + 3]).start()
+            lax.fori_loop(6, 16, step, 0)
+            lax.fori_loop(1, 6, step, 0)
             ring(0, 1)
-            lax.fori_loop(1, 16, step, 0)
 
     def finished(src, held, flip, k):
         settle(src.at[pl.ds(0, 127)], sems.at[k])
@@ -371,39 +397,74 @@
     )
 
     settle(r3, sems.at[7])
+    y = swapped(lambda quad, k: flat(r3[:, 4 * quad + k]))
     for quad in range(4):
-        x = jnp.concatenate([flat(r3[:, 4 * quad + k]) for k in range(4)], axis=1)
-        y = dot(x, lane_swap[...])
         for k in range(4):
-            dtri_f[:, k, :, 128 * quad : 128 * quad + 128] = y[:, 128 * k : 128 * k + 128].reshape(
-                8, 8, 128
-            )
-    dtri_all[core] = dtri_f[...].reshape(256, 512).astype(BF16)
+            dtri_f[:, k, :, lanes(quad)] = part_of(y, quad, k).reshape(8, 8, 128)
+    d_own = dtri_f[...].reshape(256, 512).astype(BF16)
+    dtri_all[core] = d_own
     swap2 = pltpu.make_async_remote_copy(
         dtri_all.at[core], dtri_all.at[core], sems.at[10], sems.at[11],
         device_id=beside, device_id_type=MESH,
     )
     swap2.start()
+
+    def leave_half(grad, dst, which):
+        x = jnp.concatenate(
+            [
+                jnp.concatenate(
+                    [grad[64 * k : 64 * k + 64, lanes(quad)] for k in range(4)], axis=1
+                )
+                for quad in range(2)
+            ],
+            axis=0,
+        )
+        y = dot(x, lane_swap[...])
+        for quad in range(2):
+            for k in range(4):
+                dst[:, 8 * which + 4 * quad + k] = (
+                    part_of(y, quad, k).reshape(8, 8, 128).astype(BF16)
+                )
+
+    def half_to_cells(src, dst, which, k):
+        there = dst.at[chip]
+        base = core * 8
+        spot = lax.rem(col, 8)
+
+        def ring(a, first=0):
+            block = wrap(row8 + a, 8)
+            for b in range(first, 8):
+                to_col = 8 * which + wrap(spot + b, 8)
+                start(
+                    src.at[block, to_col], there, sems.at[k], sems.at[k + 1],
+                    base + block, to_col,
+                )
+
+        def step(a, carry):
+            ring(a)
+            return carry
+
+        to_col = 8 * which + spot
+        keep_or_start(
+            jnp.logical_and(mine, to_col == col), src.at[row8, to_col], there,
+            sems.at[k], sems.at[k + 1], base + row8, to_col,
+        )
+        ring(0, 1)
+        lax.fori_loop(1, 8, step, 0)
+
+    leave_half(dot_nt(m_right[...], d_own).astype(BF16), s4l, core)
+    half_to_cells(s4l, r4l, core, 12)
     swap2.wait_recv()
+    leave_half(dot_nt(m_right[...], dtri_all[1 - core]).astype(BF16), s4l, 1 - core)
+    half_to_cells(s4l, r4l, 1 - core, 12)
     d_all = dtri_all[...].reshape(512, 512)
 
     def leave(grad, dst):
+        y = swapped(lambda quad, k: grad[64 * k : 64 * k + 64, lanes(quad)])
         for quad in range(4):
-            x = jnp.concatenate(
-                [
-                    grad[64 * k : 64 * k + 64, 128 * quad : 128 * quad + 128]
-                    for k in range(4)
-                ],
-                axis=1,
-            )
-            y = dot(x, lane_swap[...])
             for k in range(4):
-                dst[:, 4 * quad + k] = (
-                    y[:, 128 * k : 128 * k + 128].reshape(8, 8, 128).astype(BF16)
-                )
-
-    leave(dot_nt(m_right[...], d_all).astype(BF16), s4l)
-    to_cells(s4l, r4l, 12)
+                dst[:, 4 * quad + k] = part_of(y, quad, k).reshape(8, 8, 128).astype(BF16)
+
     leave(dot(m_left[...], d_all).astype(BF16), s4r)
     to_cells(s4r, r4r, 14)
     scatter(g_early, h_early, 1, 16)
@@ -444,6 +505,8 @@
     lax.fori_loop(0, 4, finish, 0, unroll=2)
     gather(h_r, o_r, a_r, 1, 24)
     lax.fori_loop(4, 8, finish, 0, unroll=2)
+    store = pltpu.make_async_copy(d_pair, d_pair_h, local_sems.at[7])
+    store.start()
 
     def collect(dst, lanes, src, base):
         for i in range(64):
@@ -466,7 +529,9 @@
         folded = folded + weighted[:, 128 * b : 128 * b + 128]
     d_gain_in[...] = jnp.sum(folded.T, axis=0, keepdims=True) / gain_in[...]
 
-    sent(s1, 0)
+    store.wait()
+    sent(s1l, 0)
+    sent(s1r, 28)
     swap.wait_send()
     sent(r2, 4)
     sent(s3, 6)
@@ -478,8 +543,31 @@
     finished(g_r, h_r, 1, 24)
 
 
+def hand_over(*refs):
+    sources, results, held, sems = refs[:5], refs[5:10], refs[10:15], refs[15]
+    pieces = []
+    for src, dst, buf in zip(sources[1:], results[1:], held[1:]):
+        pieces.append((src, dst, buf))
+    for n in range(4):
+        part = pl.ds(8 * n, 8)
+        pieces.append((sources[0].at[part], results[0].at[part], held[0].at[part]))
+    loads = []
+    stores = []
+    for n, (src, dst, buf) in enumerate(pieces):
+        loads.append(pltpu.make_async_copy(src, buf, sems.at[n]))
+        stores.append(pltpu.make_async_copy(buf, dst, sems.at[8 + n]))
+    for load in loads:
+        load.start()
+    for load, store in zip(loads, stores):
+        load.wait()
+        store.start()
+    for store in stores:
+        store.wait()
+
+
 def body(pair, pair_mask, proj_weight, out_weight, in_gain, out_gain, cotangent):
     vmem = pl.BlockSpec(memory_space=pltpu.VMEM)
+    anywhere = pl.BlockSpec(memory_space=pl.ANY)
     V = pltpu.VMEM
     tiles = V((8, 128, 128), F32)
     tiles16 = V((8, 128, 128), BF16)
@@ -487,20 +575,24 @@
     lanes16 = V((128, 1024), BF16)
     sums = (V((128, 2, 128), BF16), V((256, 2, 128), BF16), V((2, 128), BF16), V((128, 2, 128), BF16))
     scratch = [
-        V((128, 2, 8, 128), BF16), V((8, 16, 2, 8, 128), BF16),
+        V((128, 8, 128), BF16), V((128, 8, 128), BF16),
+        V((8, 16, 8, 128), BF16), V((8, 16, 8, 128), BF16),
         V((8, 16, 8, 128), BF16), V((128, 8, 128), BF16),
         V((128, 8, 128), BF16), V((8, 16, 8, 128), BF16),
         V((8, 16, 8, 128), BF16), V((8, 16, 8, 128), BF16),
         V((128, 8, 128), BF16), V((128, 8, 128), BF16),
         V((512, 512), BF16), by_tile, V((640, 128), BF16), V((128, 128), BF16),
         V((128, 128), F32), V((128, 128), F32),
-        tiles, by_tile, lanes16, tiles16, tiles16, tiles, tiles, tiles, tiles, V((8, 128), F32),
+        tiles, by_tile, lanes16, tiles16, tiles16, tiles, tiles, tiles, tiles,
         lanes16, tiles, tiles, by_tile, V((256, 512), BF16), V((256, 512), BF16),
         V((256, 512), F32), V((256, 512), BF16), V((256, 512), BF16),
         tiles, lanes16, tiles16, V((8, 4, 8, 512), F32), V((2, 256, 512), BF16),
         tiles, tiles, V((640, 1024), BF16),
         *sums, *sums, *sums,
-        pltpu.SemaphoreType.DMA((28,)),
+        V(pair.shape, BF16), V(pair_mask.shape, jnp.int32), V((128, 640), BF16), V((128, 128), BF16),
+        V((1, 128), F32), V((1, 128), F32), V(pair.shape, BF16), V(pair.shape, F32),
+        pltpu.SemaphoreType.DMA((8,)),
+        pltpu.SemaphoreType.DMA((30,)),
     ]
     outs = pl.pallas_call(
         kernel,
@@ -511,8 +603,8 @@
             jax.ShapeDtypeStruct((1, 128), F32),
             jax.ShapeDtypeStruct((1, 128), F32),
         ),
-        in_specs=[vmem] * 7,
-        out_specs=[vmem] * 5,
+        in_specs=[anywhere] * 7,
+        out_specs=[anywhere] + [vmem] * 4,
         scratch_shapes=scratch,
         name="triangle_back",
         compiler_params=pltpu.CompilerParams(collective_id=0, has_side_effects=True),
@@ -520,6 +612,14 @@
         pair, pair_mask, proj_weight, out_weight,
         in_gain.reshape(1, 128), out_gain.reshape(1, 128), cotangent,
     )
+    outs = pl.pallas_call(
+        hand_over,
+        out_shape=tuple(jax.ShapeDtypeStruct(x.shape, x.dtype) for x in outs),
+        in_specs=[anywhere] * 5,
+        out_specs=[anywhere] * 5,
+        scratch_shapes=[*(V(x.shape, x.dtype) for x in outs), pltpu.SemaphoreType.DMA((16,))],
+        name="hand_over",
+    )(*outs)
     return (*outs[:3], outs[3].reshape(128), outs[4].reshape(128))
 
 

time: 101 us -> 97 us (0.960)
  local copies, waits for them, and re-layouts: 4.53 us -> 0 us
    unnamed x13 -> x0, local copies, waits for them, and re-layouts: 4.53 us -> none
    pallas_call x0 -> x1, Pallas kernels: none -> 2.04 us  [body(): pl.pallas_call(hand_over, out_shape=tuple((jax.ShapeDtypeStruct(x.shape,...]
    pallas_call x1, Pallas kernels: 95.7 us -> 94.2 us  [body(): pl.pallas_call(kernel, out_shape=(jax.ShapeDtypeStruct(pair.shape, F32),...]
where the time goes in v5:
time: 97 us; the launch traced here: 96.9 us
  Pallas kernels  96.3 us (99%)
    pallas_call x1, Pallas kernels, body(): pl.pallas_call(kernel, out_shape=(jax.ShapeDtypeStruct(pair.shape, F32),...  94.2 us
    pallas_call x1, Pallas kernels, body(): pl.pallas_call(hand_over, out_shape=tuple((jax.ShapeDtypeStruct(x.shape,...  2.04 us

profile of v5, /device:TPU:1, one launch (start us, length us, event | category | flops | bytes accessed | tf_op | source)
XLA Modules:
  0.0 96.9 jit_solution(16825436512248190383)
XLA Ops:
  0.6 94.2 %triangle_back.1 = (f32[32,32,128]{2,1,0:T(8,128)}, f32[128,640]{1,0:T(8,128)}, f32[128,128]{1,0:T(8,128)}, f32[1,128]{1,0:T(1,128)}, f32[1,128]{1,0:T(1,128)}) custom-call(bf16[32,32,128]{2,1,0:T(8,128)(2,1)} %pair_h.1, s32[32,32]{1,0:T(8,128)} %mask_h.1, bf16[128,640]{1,0:T(8,128)(2,1)} %w_in_h.1, bf16[128,128]{1,0:T(8,128)(2,1)} %w_out_h.1, ...), custom_call_target="tpu_custom_call" | custom-call | tf_op jit(solution)/shard_map/triangle_back/pallas_call | solution.py:597
  94.9 2.0 %hand_over.1 = (f32[32,32,128]{2,1,0:T(8,128)}, f32[128,640]{1,0:T(8,128)}, f32[128,128]{1,0:T(8,128)}, f32[1,128]{1,0:T(1,128)}, f32[1,128]{1,0:T(1,128)}) custom-call(f32[32,32,128]{2,1,0:T(8,128)} %get-tuple-element.15.refs_0_, f32[128,640]{1,0:T(8,128)} %get-tuple-element.16.refs_1_, f32[128,128]{1,0:T(8,128)} %get-tuple-element.17.refs_2_, ...), custom_call_target="tpu_custom_call" | custom-call | tf_op jit(solution)/shard_map/hand_over/pallas_call | solution.py:615

commit v6 on v5

--- a/solution.py
+++ b/solution.py
@@ -64,7 +64,7 @@
 def kernel(
     pair_h, mask_h, w_in_h, w_out_h, gain_in_h, gain_out_h, cot_h,
     d_pair_h, d_w_in, d_w_out, d_gain_in, d_gain_out,
-    s1l, s1r, r1l, r1r, s2, r2, s3, r3, s4l, s4r, r4l, r4r,
+    s1l, s1r, r1l, r1r, s2a, s2b, r2a, r2b, s3a, s3b, r3a, r3b, s4l, s4r, r4l, r4r,
     lane_swap, cell_mask, w_in_t, w_out_t, gi, go,
     zhat, s_z, zn, left, right, a_left, b_left, a_right, b_right,
     dproj, upper, h, h_mean, m_left, m_right, part, part_out, part_in,
@@ -292,10 +292,12 @@
     y = swapped(lambda quad, k: product[:, k, :, lanes(quad)].reshape(64, 128).astype(BF16))
     for quad in range(4):
         for k in range(4):
-            s2[:, 4 * quad + k] = part_of(y, quad, k).reshape(8, 8, 128).astype(BF16)
-
-    to_cells(s2, r2, 4)
-    settle(r2, sems.at[5])
+            block = part_of(y, quad, k).reshape(8, 8, 128)
+            s2a[:, 4 * quad + k] = block[:, 0:4].astype(BF16)
+            s2b[:, 4 * quad + k] = block[:, 4:8].astype(BF16)
+
+    to_cells(s2a, r2a, 4)
+    to_cells(s2b, r2b, 30)
 
     def to_tile_rows(src, dst):
         for g in range(8):
@@ -304,7 +306,6 @@
             for j in range(8):
                 dst[j, 16 * g : 16 * g + 16, :] = y[16 * j : 16 * j + 16]
 
-    to_tile_rows(lambda g: r2[16 * g : 16 * g + 16], tri)
 
     def middle(j, carry):
         that, inverse = normalize(tri[j])
@@ -316,11 +317,26 @@
         dtri[j] = d_t.astype(BF16)
         return carry
 
-    lax.fori_loop(0, 8, middle, 0, unroll=2)
-
-    for g in range(8):
-        s3[16 * g : 16 * g + 16] = to_blocks(dtri, g)
-    to_chips(s3, r3, 6)
+    to_half_block = jnp.where(c_i == (r_i & 3) * 32 + (r_i >> 2), 1.0, 0.0).astype(BF16)
+    to_half_tiles = jnp.where(c_i == (r_i & 31) * 4 + (r_i >> 5), 1.0, 0.0).astype(BF16)
+
+    def middle_half(landed, leaving, landed_sem, first):
+        settle(landed, sems.at[landed_sem])
+        for g in range(4):
+            channels = slice(32 * g, 32 * g + 32)
+            y = dot(to_half_tiles, landed[channels].astype(F32).reshape(128, 128).astype(BF16))
+            for j in range(4):
+                tri[first + j, channels, :] = y[32 * j : 32 * j + 32]
+        lax.fori_loop(first, first + 4, middle, 0, unroll=2)
+        for g in range(4):
+            channels = slice(32 * g, 32 * g + 32)
+            y = dot(to_half_block, dtri[first : first + 4, channels, :].reshape(128, 128))
+            leaving[channels] = y.reshape(32, 4, 128).astype(BF16)
+
+    middle_half(r2a, s3a, 5, 0)
+    to_chips(s3a, r3a, 6)
+    middle_half(r2b, s3b, 31, 4)
+    to_chips(s3b, r3b, 32)
 
     def fill(dst, value):
         rows = value.astype(BF16)
@@ -396,8 +412,14 @@
         ),
     )
 
-    settle(r3, sems.at[7])
-    y = swapped(lambda quad, k: flat(r3[:, 4 * quad + k]))
+    settle(r3a, sems.at[7])
+    settle(r3b, sems.at[33])
+
+    def joined(q):
+        both = jnp.concatenate([r3a[:, q].astype(F32), r3b[:, q].astype(F32)], axis=1)
+        return both.reshape(64, 128).astype(BF16)
+
+    y = swapped(lambda quad, k: joined(4 * quad + k))
     for quad in range(4):
         for k in range(4):
             dtri_f[:, k, :, lanes(quad)] = part_of(y, quad, k).reshape(8, 8, 128)
@@ -533,8 +555,10 @@
     sent(s1l, 0)
     sent(s1r, 28)
     swap.wait_send()
-    sent(r2, 4)
-    sent(s3, 6)
+    sent(r2a, 4)
+    sent(r2b, 30)
+    sent(s3a, 6)
+    sent(s3b, 32)
     swap2.wait_send()
     sent(r4l, 12)
     sent(r4r, 14)
@@ -577,8 +601,10 @@
     scratch = [
         V((128, 8, 128), BF16), V((128, 8, 128), BF16),
         V((8, 16, 8, 128), BF16), V((8, 16, 8, 128), BF16),
-        V((8, 16, 8, 128), BF16), V((128, 8, 128), BF16),
-        V((128, 8, 128), BF16), V((8, 16, 8, 128), BF16),
+        V((8, 16, 4, 128), BF16), V((8, 16, 4, 128), BF16),
+        V((128, 4, 128), BF16), V((128, 4, 128), BF16),
+        V((128, 4, 128), BF16), V((128, 4, 128), BF16),
+        V((8, 16, 4, 128), BF16), V((8, 16, 4, 128), BF16),
         V((8, 16, 8, 128), BF16), V((8, 16, 8, 128), BF16),
         V((128, 8, 128), BF16), V((128, 8, 128), BF16),
         V((512, 512), BF16), by_tile, V((640, 128), BF16), V((128, 128), BF16),
@@ -592,7 +618,7 @@
         V(pair.shape, BF16), V(pair_mask.shape, jnp.int32), V((128, 640), BF16), V((128, 128), BF16),
         V((1, 128), F32), V((1, 128), F32), V(pair.shape, BF16), V(pair.shape, F32),
         pltpu.SemaphoreType.DMA((8,)),
-        pltpu.SemaphoreType.DMA((30,)),
+        pltpu.SemaphoreType.DMA((34,)),
     ]
     outs = pl.pallas_call(
         kernel,

time: 97 us -> 94.8 us (0.977)
  Pallas kernels: 96.3 us -> 94 us
    pallas_call x1, Pallas kernels: 94.2 us -> 92 us  [body(): pl.pallas_call(kernel, out_shape=(jax.ShapeDtypeStruct(pair.shape, F32),...]
where the time goes in v6:
time: 94.8 us; the launch traced here: 94.7 us
  Pallas kernels  94 us (99%)
    pallas_call x1, Pallas kernels, body(): pl.pallas_call(kernel, out_shape=(jax.ShapeDtypeStruct(pair.shape, F32),...  92 us
    pallas_call x1, Pallas kernels, body(): pl.pallas_call(hand_over, out_shape=tuple((jax.ShapeDtypeStruct(x.shape,...  2.04 us

profile of v6, /device:TPU:1, one launch (start us, length us, event | category | flops | bytes accessed | tf_op | source)
XLA Modules:
  0.0 94.7 jit_solution(6129778916511359469)
XLA Ops:
  0.6 92.0 %triangle_back.1 = (f32[32,32,128]{2,1,0:T(8,128)}, f32[128,640]{1,0:T(8,128)}, f32[128,128]{1,0:T(8,128)}, f32[1,128]{1,0:T(1,128)}, f32[1,128]{1,0:T(1,128)}) custom-call(bf16[32,32,128]{2,1,0:T(8,128)(2,1)} %pair_h.1, s32[32,32]{1,0:T(8,128)} %mask_h.1, bf16[128,640]{1,0:T(8,128)(2,1)} %w_in_h.1, bf16[128,128]{1,0:T(8,128)(2,1)} %w_out_h.1, ...), custom_call_target="tpu_custom_call" | custom-call | tf_op jit(solution)/shard_map/triangle_back/pallas_call | solution.py:623
  92.6 2.0 %hand_over.1 = (f32[32,32,128]{2,1,0:T(8,128)}, f32[128,640]{1,0:T(8,128)}, f32[128,128]{1,0:T(8,128)}, f32[1,128]{1,0:T(1,128)}, f32[1,128]{1,0:T(1,128)}) custom-call(f32[32,32,128]{2,1,0:T(8,128)} %get-tuple-element.15.refs_0_, f32[128,640]{1,0:T(8,128)} %get-tuple-element.16.refs_1_, f32[128,128]{1,0:T(8,128)} %get-tuple-element.17.refs_2_, ...), custom_call_target="tpu_custom_call" | custom-call | tf_op jit(solution)/shard_map/hand_over/pallas_call | solution.py:641

commit v7 on v6

--- a/solution.py
+++ b/solution.py
@@ -568,22 +568,12 @@
 
 
 def hand_over(*refs):
-    sources, results, held, sems = refs[:5], refs[5:10], refs[10:15], refs[15]
-    pieces = []
-    for src, dst, buf in zip(sources[1:], results[1:], held[1:]):
-        pieces.append((src, dst, buf))
-    for n in range(4):
-        part = pl.ds(8 * n, 8)
-        pieces.append((sources[0].at[part], results[0].at[part], held[0].at[part]))
-    loads = []
-    stores = []
-    for n, (src, dst, buf) in enumerate(pieces):
-        loads.append(pltpu.make_async_copy(src, buf, sems.at[n]))
-        stores.append(pltpu.make_async_copy(buf, dst, sems.at[8 + n]))
-    for load in loads:
-        load.start()
-    for load, store in zip(loads, stores):
-        load.wait()
+    sems = refs[10]
+    stores = [
+        pltpu.make_async_copy(src, dst, sems.at[n])
+        for n, (src, dst) in enumerate(zip(refs[:5], refs[5:10]))
+    ]
+    for store in stores:
         store.start()
     for store in stores:
         store.wait()
@@ -629,21 +619,27 @@
             jax.ShapeDtypeStruct((1, 128), F32),
             jax.ShapeDtypeStruct((1, 128), F32),
         ),
-        in_specs=[anywhere] * 7,
+        in_specs=[pl.BlockSpec(memory_space=pltpu.HBM)] * 7,
         out_specs=[anywhere] + [vmem] * 4,
         scratch_shapes=scratch,
         name="triangle_back",
-        compiler_params=pltpu.CompilerParams(collective_id=0, has_side_effects=True),
+        compiler_params=pltpu.CompilerParams(collective_id=0, has_side_effects=True, vmem_limit_bytes=24 * 2**20),
     )(
-        pair, pair_mask, proj_weight, out_weight,
-        in_gain.reshape(1, 128), out_gain.reshape(1, 128), cotangent,
+        *(
+            pltpu.with_memory_space_constraint(x, pltpu.HBM)
+            for x in (
+                pair, pair_mask, proj_weight, out_weight,
+                in_gain.reshape(1, 128), out_gain.reshape(1, 128), cotangent,
+            )
+        )
     )
     outs = pl.pallas_call(
         hand_over,
         out_shape=tuple(jax.ShapeDtypeStruct(x.shape, x.dtype) for x in outs),
         in_specs=[anywhere] * 5,
-        out_specs=[anywhere] * 5,
-        scratch_shapes=[*(V(x.shape, x.dtype) for x in outs), pltpu.SemaphoreType.DMA((16,))],
+        out_specs=[pl.BlockSpec(memory_space=pltpu.HBM)] * 5,
+        scratch_shapes=[pltpu.SemaphoreType.DMA((5,))],
+        compiler_params=pltpu.CompilerParams(vmem_limit_bytes=2 * 2**20),
         name="hand_over",
     )(*outs)
     return (*outs[:3], outs[3].reshape(128), outs[4].reshape(128))

time: 94.8 us -> 92.9 us (0.980)
  Pallas kernels: 94 us -> 92.1 us
    pallas_call x1, Pallas kernels: 2.04 us -> 0.96 us  [body(): pl.pallas_call(hand_over, out_shape=tuple((jax.ShapeDtypeStruct(x.shape,...]
where the time goes in v7:
time: 92.9 us; the launch traced here: 92.8 us
  Pallas kernels  92.1 us (99%)
    pallas_call x1, Pallas kernels, body(): pl.pallas_call(kernel, out_shape=(jax.ShapeDtypeStruct(pair.shape, F32),...  91.2 us

profile of v7, /device:TPU:1, one launch (start us, length us, event | category | flops | bytes accessed | tf_op | source)
XLA Modules:
  0.0 92.8 jit_solution(14316724546174772261)
XLA Ops:
  0.6 91.2 %triangle_back.1 = (f32[32,32,128]{2,1,0:T(8,128)S(1)}, f32[128,640]{1,0:T(8,128)S(1)}, f32[128,128]{1,0:T(8,128)S(1)}, f32[1,128]{1,0:T(1,128)S(1)}, f32[1,128]{1,0:T(1,128)S(1)}) custom-call(bf16[32,32,128]{2,1,0:T(8,128)(2,1)} %pair_h.1, s32[32,32]{1,0:T(8,128)} %mask_h.1, bf16[128,640]{1,0:T(8,128)(2,1)} %w_in_h.1, bf16[128,128]{1,0:T(8,128)(2,1)} %w_out_h.1, ...), custom_call_target="tpu_custom_call" | custom-call | tf_op jit(solution)/shard_map/triangle_back/pallas_call | solution.py:613
  91.8 1.0 %hand_over.1 = (f32[32,32,128]{2,1,0:T(8,128)}, f32[128,640]{1,0:T(8,128)}, f32[128,128]{1,0:T(8,128)}, f32[1,128]{1,0:T(1,128)}, f32[1,128]{1,0:T(1,128)}) custom-call(f32[32,32,128]{2,1,0:T(8,128)S(1)} %get-tuple-element.15.refs_0_, f32[128,640]{1,0:T(8,128)S(1)} %get-tuple-element.16.refs_1_, f32[128,128]{1,0:T(8,128)S(1)} %get-tuple-element.17.refs_2_, ...), custom_call_target="tpu_custom_call" | custom-call | tf_op jit(solution)/shard_map/hand_over/pallas_call | solution.py:636

commit v8 on v7

--- a/solution.py
+++ b/solution.py
@@ -489,7 +489,6 @@
 
     leave(dot(m_left[...], d_all).astype(BF16), s4r)
     to_cells(s4r, r4r, 14)
-    scatter(g_early, h_early, 1, 16)
 
     def back(grad, value, slope, base):
         def step(j, carry):
@@ -505,6 +504,7 @@
     back(grad_l, a_left, b_left, 0)
     fill(g_l, dot_nt(zn[...], dlin[0:256]))
     scatter(g_l, h_l, 0, 20)
+    scatter(g_early, h_early, 1, 16)
 
     settle(r4r, sems.at[15])
     to_tile_rows(lambda g: r4r[16 * g : 16 * g + 16], grad_r)

time: 92.9 us -> 92.7 us (level)
  no operation moved by 1% of the time
where the time goes in v8:
time: 92.7 us; the launch traced here: 92.6 us
  Pallas kernels  92 us (99%)
    pallas_call x1, Pallas kernels, body(): pl.pallas_call(kernel, out_shape=(jax.ShapeDtypeStruct(pair.shape, F32),...  91 us

profile of v8, /device:TPU:1, one launch (start us, length us, event | category | flops | bytes accessed | tf_op | source)
XLA Modules:
  0.0 92.6 jit_solution(3889902660742999406)
XLA Ops:
  0.6 91.0 %triangle_back.1 = (f32[32,32,128]{2,1,0:T(8,128)S(1)}, f32[128,640]{1,0:T(8,128)S(1)}, f32[128,128]{1,0:T(8,128)S(1)}, f32[1,128]{1,0:T(1,128)S(1)}, f32[1,128]{1,0:T(1,128)S(1)}) custom-call(bf16[32,32,128]{2,1,0:T(8,128)(2,1)} %pair_h.1, s32[32,32]{1,0:T(8,128)} %mask_h.1, bf16[128,640]{1,0:T(8,128)(2,1)} %w_in_h.1, bf16[128,128]{1,0:T(8,128)(2,1)} %w_out_h.1, ...), custom_call_target="tpu_custom_call" | custom-call | tf_op jit(solution)/shard_map/triangle_back/pallas_call | solution.py:613
  91.6 1.0 %hand_over.1 = (f32[32,32,128]{2,1,0:T(8,128)}, f32[128,640]{1,0:T(8,128)}, f32[128,128]{1,0:T(8,128)}, f32[1,128]{1,0:T(1,128)}, f32[1,128]{1,0:T(1,128)}) custom-call(f32[32,32,128]{2,1,0:T(8,128)S(1)} %get-tuple-element.15.refs_0_, f32[128,640]{1,0:T(8,128)S(1)} %get-tuple-element.16.refs_1_, f32[128,128]{1,0:T(8,128)S(1)} %get-tuple-element.17.refs_2_, ...), custom_call_target="tpu_custom_call" | custom-call | tf_op jit(solution)/shard_map/hand_over/pallas_call | solution.py:636
